TPU v7x, 256 devices: a whole 4x4x8 slice. The times are simulated.
256 devices in a mesh: rep: 16 (over z, core), rows: 16 (over y, x).
Axes of the slice: x: 4, y: 4, z: 8, core: 2. Of those that a mesh axis runs over, the one named last changes fastest.
Arguments:
- weights: bfloat16 [7168, 2048], P('rows'), may hold values from -6 to 6
- momentum: float32 [16, 7168, 2048], P('rep', 'rows'), may hold values from -8 to 8
- gradient: bfloat16 [16, 7168, 2048], P('rep', 'rows'), may hold values from -8 to 8
- right_factor: float32 [2048, 512], P('rows'), may hold values from -6 to 6
Outputs:
- new_weights: bfloat16 [7168, 2048], P('rows')
- new_momentum: float32 [16, 7168, 2048], P('rep', 'rows')
- new_right: float32 [2048, 512], P('rows')
All inputs are finite; a program needn't handle non-finite values.
Results may differ from a plain program's by a relative error of at most 0.019.
Values may be sent and summed in bfloat16 or wider, within the bound.
No kernel may reach another device: no remote copies, remote signals or barrier semaphores. Data moves between devices by JAX's collectives and lax.ppermute only.
A program may use at most 64 MiB of HBM per device.

v0:
```python
import jax
import jax.numpy as jnp
from jax import lax
from jax.experimental import pallas as pl
from jax.experimental.pallas import tpu as pltpu
from jax.sharding import Mesh
from jax.sharding import PartitionSpec as P

M = 7168
N = 2048
ROWS = ("y", "x")
REP = ("z", "c")
SWAP = [(0, 1), (1, 0)]
PANEL = 128
HI = lax.Precision.HIGHEST
THREE = lax.Precision.HIGH
f32 = jnp.float32
bf16 = jnp.bfloat16

momentum_keep = 0.05
learn_rate = 0.5
tiny = 1e-06


def eliminate(block):
    sub = lax.broadcasted_iota(jnp.int32, (8, PANEL), 0)
    lane = lax.broadcasted_iota(jnp.int32, (8, PANEL), 1)
    tiles = PANEL // 8
    rows = [block[8 * r : 8 * r + 8, :] for r in range(tiles)]
    pivots = []
    for m in range(tiles):
        here = (lane >= 8 * m) & (lane < 8 * m + 8)
        at = [8 * m + k for k in range(8)]
        cols = [jnp.broadcast_to(rows[m][:, i : i + 1], (8, PANEL)) for i in at]
        low = jnp.where(here, jnp.where(lane - 8 * m == sub, 1.0, 0.0), rows[m])
        full = low
        pivot = jnp.zeros((8, PANEL), f32)
        for k in range(8):
            col = cols[k]
            head = jnp.broadcast_to(col[k : k + 1, :], (8, PANEL))
            inv = 1.0 / head
            pivot = jnp.where(sub == k, head, pivot)

            def step(value):
                row = jnp.broadcast_to(value[k : k + 1, :], (8, PANEL)) * inv
                return jnp.where(sub == k, row, value - col * row)

            if k < 7:
                row = jnp.broadcast_to(low[k : k + 1, :], (8, PANEL)) * inv
                low = jnp.where(sub > k, low - col * row, low)
            cols = [step(other) if n > k else other for n, other in enumerate(cols)]
            full = step(full)
        solved = [jnp.broadcast_to(full[k : k + 1, :], (8, PANEL)) for k in range(8)]
        for r in range(m + 1, tiles):
            parts = [
                jnp.broadcast_to(rows[r][:, i : i + 1], (8, PANEL)) * solved[k]
                for k, i in enumerate(at)
            ]
            while len(parts) > 1:
                parts = [parts[n] + parts[n + 1] for n in range(0, len(parts), 2)]
            rows[r] = jnp.where(here, 0.0, rows[r]) - parts[0]
        rows[m] = low
        pivots.append(pivot)
    return jnp.concatenate(rows, 0), jnp.concatenate(pivots, 0)


def exact_dot(a, b, dim=1, other=0, precision=HI):
    dims = (((dim,), (other,)), ((), ()))
    return lax.dot_general(a, b, dims, precision=precision, preferred_element_type=f32)


def panels(work_ref, out_ref, which):
    size = out_ref.shape[0]
    row = lax.broadcasted_iota(jnp.int32, (PANEL, PANEL), 0)
    lane = lax.broadcasted_iota(jnp.int32, (PANEL, PANEL), 1)
    for p in which:
        a, b = p * PANEL, (p + 1) * PANEL
        packed, pivot = eliminate(work_ref[a:b, a:b])
        lower = jnp.where(lane <= row, packed, 0.0)
        scale = lax.rsqrt(pivot)
        out_ref[a:b, a:b] = lower * scale
        if p > 0:
            left = exact_dot(lower, work_ref[a:b, :a])
            out_ref[a:b, :a] = left * jnp.concatenate([scale] * p, 1)
        if b < size:
            right = exact_dot(lower, work_ref[a:b, b:])
            out_ref[a:b, b:] = jnp.zeros((PANEL, size - b), f32)
            down = right * jnp.concatenate([1.0 / pivot] * ((size - b) // PANEL), 1)
            work_ref[b:, b:] = work_ref[b:, b:] - exact_dot(down, right, 0)
            work_ref[b:, a:b] = -exact_dot(down, lower, 0)
            if p > 0:
                work_ref[b:, :a] = work_ref[b:, :a] - exact_dot(down, left, 0)


def upper_kernel(first_ref, second_ref, out_ref):
    size = out_ref.shape[0]
    half = size // 2
    out_ref[:half, :half] = first_ref[:, :half]
    out_ref[:half, half : half + PANEL] = first_ref[:, half:]
    out_ref[:half, half + PANEL :] = second_ref[:, half:]
    out_ref[half:, half:] = second_ref[:, :half]
    panels(out_ref, out_ref, range(size // PANEL // 2))


def lower_kernel(in_ref, out_ref):
    size = out_ref.shape[0]
    out_ref[...] = in_ref[...]
    panels(out_ref, out_ref, range(size // PANEL // 2, size // PANEL))


def half_factor(kernel, size, *operands):
    space = pl.BlockSpec(memory_space=pltpu.VMEM)
    return pl.pallas_call(
        kernel,
        out_shape=jax.ShapeDtypeStruct((size, size), f32),
        in_specs=[space] * len(operands),
        out_specs=space,
        cost_estimate=pl.CostEstimate(
            flops=6_000_000_000, bytes_accessed=2_000_000, transcendentals=1000
        ),
    )(*operands)


def exchange(value, axes):
    return lax.all_to_all(value, axes, 0, 0, tiled=True)


def gather(value, axes):
    size = lax.axis_size(axes)
    return exchange(jnp.broadcast_to(value[None], (size, *value.shape)), axes)


def partner(value):
    return lax.ppermute(value, "c", SWAP)


def in_order(mine, theirs, core):
    first = jnp.where(core == 0, mine, theirs)
    second = jnp.where(core == 0, theirs, mine)
    return first, second


def per_device(weights, momentum, gradient, right_factor):
    core = lax.axis_index("c")
    depth = lax.axis_size("z")
    blocks = lax.axis_size(ROWS)
    groups = depth * lax.axis_size("c")
    me = lax.axis_index(ROWS)
    rank = right_factor.shape[1]
    half = rank // 2
    rows, columns = momentum.shape[1:]

    right_half = lax.dynamic_slice_in_dim(right_factor, core * half, half, 1).astype(bf16)
    right_half = gather(right_half, ROWS).reshape(columns, half)

    combined = momentum[0] + gradient[0].astype(f32)
    mine = combined.astype(bf16)
    theirs = partner(mine)

    left = jnp.dot(mine, right_half, preferred_element_type=f32) + jnp.dot(
        theirs, right_half, preferred_element_type=f32
    )
    left = exchange(left.astype(bf16).reshape(depth, rows // depth, half), "z")
    left = left.astype(f32).sum(0) / groups
    left = gather(left, "z").reshape(rows, half)
    first, second = in_order(left, partner(left), core)
    left_mean = jnp.concatenate([first, second], 1)

    own = exact_dot(left, left, 0)
    cross = exact_dot(first, lax.dynamic_slice_in_dim(second, core * PANEL, PANEL, 1), 0)
    gram = jnp.concatenate([own, cross], 1)
    gram = exchange(gram.reshape(blocks, half // blocks, half + PANEL), ROWS)
    gram = gram.sum(0)
    gram = gather(gram, ROWS).reshape(half, half + PANEL)
    mirrored = partner(gram)
    mirrored = in_order(gram, mirrored, core)
    inverse = half_factor(upper_kernel, rank, *mirrored)
    inverse = half_factor(lower_kernel, rank, inverse)

    wide = columns // 2
    place = lax.axis_index("z")
    width = wide // depth
    terms = []
    for shift in range(depth):
        at = core * wide + lax.rem(place + shift, depth) * width
        term = lax.dynamic_slice_in_dim(mine, at, width, 1).astype(f32)
        term = (term + lax.dynamic_slice_in_dim(theirs, at, width, 1).astype(f32)).astype(bf16)
        if shift > 0:
            term, _ = lax.optimization_barrier((term, left))
            term = lax.ppermute(term, "z", [(n, (n + shift) % depth) for n in range(depth)])
        terms.append(term)
    terms, _ = lax.optimization_barrier((terms, gram))
    mean = sum(term.astype(f32) for term in terms) / groups
    crossed = exact_dot(mean, left_mean, 0, 0, THREE)
    crossed = exchange(crossed.reshape(blocks, -1, rank), ROWS)
    crossed = crossed.sum(0)
    crossed = gather(crossed, "z").reshape(-1, rank)

    turn = (((1,), (1,)), ((), ()))
    part = exact_dot(crossed, inverse, 1, 1, THREE)
    part = gather(part.astype(bf16), ROWS)
    left_half = exact_dot(left_mean, inverse, 1, 1, THREE).astype(bf16)
    right_mean = jnp.stack(in_order(part, partner(part), core), 0)
    right_mean = right_mean.reshape(2, blocks, depth, -1, rank)
    right_mean = jnp.moveaxis(right_mean, 2, 1).reshape(columns, rank)

    squares = jnp.sum(jnp.square(right_mean.astype(f32)), axis=0)
    norm = jnp.sqrt(squares / columns + tiny)
    short = columns // blocks
    new_right = lax.dynamic_slice_in_dim(right_mean, me * short, short, 0).astype(f32) / norm
    scaled = (right_mean.astype(f32) / norm).astype(bf16)
    feedback = lax.dot_general(left_half, right_mean, turn, preferred_element_type=f32)
    update = lax.dot_general(left_half, scaled, turn, preferred_element_type=f32)
    new_momentum = combined - momentum_keep * feedback
    new_weights = (weights.astype(f32) - learn_rate * jnp.sqrt(M / N) * update).astype(bf16)
    return (new_weights, new_momentum[None], new_right)


def solution(mesh):
    split = Mesh(mesh.devices.reshape(mesh.shape["rep"] // 2, 2, 4, 4), ("z", "c", "y", "x"))
    in_specs = (P(ROWS, None), P(REP, ROWS, None), P(REP, ROWS, None), P(ROWS, None))
    out_specs = (P(ROWS, None), P(REP, ROWS, None), P(ROWS, None))

    return jax.shard_map(
        per_device, mesh=split, in_specs=in_specs, out_specs=out_specs, check_vma=False
    )
```

profile of v0, /device:TPU:1, one launch (start us, length us, event | category | flops | bytes accessed | tf_op | source)
XLA Modules:
  0.0 211.1 jit_solution(14777453719310876851)
XLA Ops:
  0.6 0.0 copy-start
  0.6 4.5 %bitcast_convert_fusion = bf16[448,2048]{1,0:T(8,128)(2,1)} fusion(f32[1,448,2048]{2,1,0:T(8,128)} %param.5, bf16[1,448,2048]{2,1,0:T(8,128)(2,1)} %param.6), kind=kLoop, calls=%fused_computation.3 | loop fusion | flops 2752512 | bytes 7340032 | tf_op jit(solution)/shard_map/convert_element_type | solution.py:157
  5.1 3.2 %collective-permute-start = (bf16[448,2048]{1,0:T(8,128)(2,1)}, bf16[448,2048]{1,0:T(8,128)(2,1)}, u32[]{:S(2)}, u32[]{:S(2)}) collective-permute-start(bf16[448,2048]{1,0:T(8,128)(2,1)} %bitcast_convert_fusion), channel_id=1, source_target_pairs={{0,16},{16,0},{1,17},{17,1},{2,18},{18,2},{3,19},{19,3},{4,20},{20... | collective-permute-start | bytes 5505032 | tf_op jit(solution)/shard_map/ppermute | solution.py:134
  8.3 0.0 copy-done
  8.4 0.1 broadcast_in_dim.12
  8.5 21.4 %all_to_all.40 = bf16[16,128,256]{2,1,0:T(8,128)(2,1)S(1)} all-to-all(bf16[16,128,256]{2,1,0:T(8,128)(2,1)S(1)} %broadcast_in_dim.12), channel_id=1, replica_groups=mesh['z'=8,'c'=2,'y'=4,'x'=4] {'y','x'}, dimensions={0} | all-to-all | bytes 2097152 | tf_op jit(solution)/shard_map/all_to_all | solution.py:125
  29.8 0.0 copy-done.2
  29.8 2.7 %fusion.1 = f32[448,256]{1,0:T(8,128)S(1)} fusion(bf16[2048,256]{1,0:T(8,128)(2,1)S(1)} %bitcast.50, f32[1,448,2048]{2,1,0:T(8,128)} %param.5, bf16[1,448,2048]{2,1,0:T(8,128)(2,1)S(1)} %copy-done.2), kind=kOutput, calls=%fused_computation.8 | convolution fusion | flops 472514560 | bytes 7012352 | tf_op jit(solution)/shard_map/dot_general | solution.py:160
  32.6 0.0 collective-permute-done
  32.6 2.1 %fusion.4 = bf16[448,256]{1,0:T(8,128)(2,1)S(1)} fusion(f32[448,256]{1,0:T(8,128)S(1)} %fusion.1, bf16[448,2048]{1,0:T(8,128)(2,1)} %collective-permute-done, bf16[2048,256]{1,0:T(8,128)(2,1)S(1)} %bitcast.51), kind=kOutput, calls=%fused_computation.13 | convolution fusion | flops 469991424 | bytes 3571712 | tf_op jit(solution)/shard_map/dot_general | solution.py:160
  34.7 16.9 %all_to_all.41 = bf16[8,56,256]{2,1,0:T(8,128)(2,1)S(1)} all-to-all(bf16[8,56,256]{2,1,0:T(8,128)(2,1)S(1)} %bitcast.54), channel_id=1, replica_groups=mesh['z'=8,'c'=2,'y'=4,'x'=4] {'z'}, dimensions={0} | all-to-all | bytes 458752 | tf_op jit(solution)/shard_map/all_to_all | solution.py:125
  51.7 14.7 %all_to_all.42 = f32[8,56,256]{2,1,0:T(8,128)S(1)} all-to-all(f32[8,56,256]{2,1,0:T(8,128)S(1)} %broadcast_in_dim.13), channel_id=1, replica_groups=mesh['z'=8,'c'=2,'y'=4,'x'=4] {'z'}, dimensions={0} | all-to-all | bytes 917504 | tf_op jit(solution)/shard_map/all_to_all | solution.py:125
  66.3 4.8 %collective-permute-start.1 = (f32[448,256]{1,0:T(8,128)S(1)}, f32[448,256]{1,0:T(8,128)}, u32[]{:S(2)}, u32[]{:S(2)}) collective-permute-start(f32[448,256]{1,0:T(8,128)S(1)} %bitcast.49), channel_id=1, source_target_pairs={{0,16},{16,0},{1,17},{17,1},{2,18},{18,2},{3,19},{19,3},{4,20},{20... | collective-permute-start | bytes 1376264 | tf_op jit(solution)/shard_map/ppermute | solution.py:134
  71.1 1.0 convolution_bitcast_fusion
  72.1 0.6 collective-permute-done.1
  72.7 1.1 broadcast_select_fusion
  73.8 0.6 fusion.21
  74.5 0.9 copy.8
  75.4 4.0 %all-to-all-start.3 = ((f32[16,16,384]{2,1,0:T(8,128)}), f32[16,16,384]{2,1,0:T(8,128)S(1)}, u32[]{:S(2)}, u32[]{:S(2)}) async-start(f32[16,16,384]{2,1,0:T(8,128)} %bitcast.52), calls=%async_computation.3 | async-start | bytes 786432 | tf_op jit(solution)/shard_map/all_to_all | solution.py:125
  79.4 9.5 %all-to-all-done.3 = f32[16,16,384]{2,1,0:T(8,128)S(1)} async-done(((f32[16,16,384]{2,1,0:T(8,128)}), f32[16,16,384]{2,1,0:T(8,128)S(1)}, u32[]{:S(2)}, u32[]{:S(2)}) %all-to-all-start.3) | async-done | bytes 393248 | tf_op jit(solution)/shard_map/all_to_all | solution.py:125
  88.9 0.8 broadcast_in_dim.14
  89.7 3.6 %all-to-all-start.4 = ((f32[16,16,384]{2,1,0:T(8,128)}), f32[16,16,384]{2,1,0:T(8,128)S(1)}, u32[]{:S(2)}, u32[]{:S(2)}) async-start(f32[16,16,384]{2,1,0:T(8,128)} %broadcast_in_dim.14), calls=%async_computation.4 | async-start | bytes 786432 | tf_op jit(solution)/shard_map/all_to_all | solution.py:125
  93.3 2.6 %add_convert_fusion = (bf16[448,128]{1,0:T(8,128)(2,1)}, bf16[448,128]{1,0:T(8,128)(2,1)}, bf16[448,128]{1,0:T(8,128)(2,1)}, bf16[448,128]{1,0:T(8,128)(2,1)}, b...) fusion(bf16[448,2048]{1,0:T(8,128)(2,1)} %collective-permute-do, ...), kind=kLoop, calls=%fused_computation.39 | loop fusion | flops 1835008 | bytes 2752544 | tf_op jit(solution)/shard_map/convert_element_type | solution.py:187
  95.9 0.3 collective-permute-start.3
  96.2 0.1 collective-permute-start.4
  96.2 2.0 collective-permute-start.5
  98.3 3.3 %collective-permute-start.6 = (bf16[448,128]{1,0:T(8,128)(2,1)}, bf16[448,128]{1,0:T(8,128)(2,1)}, u32[]{:S(2)}, u32[]{:S(2)}) collective-permute-start(bf16[448,128]{1,0:T(8,128)(2,1)} %get-tuple-element.21), channel_id=1, source_target_pairs={{0,128},{32,160},{64,192},{96,224},{128,0},{160,32},{192,64},{224,... | collective-permute-start | bytes 344072 | tf_op jit(solution)/shard_map/ppermute | solution.py:190
  101.6 0.9 collective-permute-start.7
  102.6 0.0 collective-permute-done.3
  102.6 2.8 %collective-permute-start.8 = (bf16[448,128]{1,0:T(8,128)(2,1)}, bf16[448,128]{1,0:T(8,128)(2,1)}, u32[]{:S(2)}, u32[]{:S(2)}) collective-permute-start(bf16[448,128]{1,0:T(8,128)(2,1)} %get-tuple-element.23), channel_id=1, source_target_pairs={{0,192},{32,224},{64,0},{96,32},{128,64},{160,96},{192,128},{224,1... | collective-permute-start | bytes 344072 | tf_op jit(solution)/shard_map/ppermute | solution.py:190
  105.4 0.0 collective-permute-done.4
  105.4 1.4 collective-permute-start.9
  106.8 0.0 copy-done.4
  106.8 7.9 %collective-permute-done.5 = bf16[448,128]{1,0:T(8,128)(2,1)} collective-permute-done((bf16[448,128]{1,0:T(8,128)(2,1)S(1)}, bf16[448,128]{1,0:T(8,128)(2,1)}, u32[]{:S(2)}, u32[]{:S(2)}) %collective-permute-start.5) | collective-permute-done | bytes 114720 | tf_op jit(solution)/shard_map/ppermute | solution.py:190
  114.7 0.0 all-to-all-done.4
  114.7 2.0 collective-permute-start.2
  116.7 0.0 collective-permute-done.6
  116.7 0.0 collective-permute-done.7
  116.7 3.5 %collective-permute-done.8 = bf16[448,128]{1,0:T(8,128)(2,1)} collective-permute-done((bf16[448,128]{1,0:T(8,128)(2,1)}, bf16[448,128]{1,0:T(8,128)(2,1)}, u32[]{:S(2)}, u32[]{:S(2)}) %collective-permute-start.8) | collective-permute-done | bytes 114720 | tf_op jit(solution)/shard_map/ppermute | solution.py:190
  120.2 2.9 %collective-permute-done.9 = bf16[448,128]{1,0:T(8,128)(2,1)} collective-permute-done((bf16[448,128]{1,0:T(8,128)(2,1)}, bf16[448,128]{1,0:T(8,128)(2,1)}, u32[]{:S(2)}, u32[]{:S(2)}) %collective-permute-start.9) | collective-permute-done | bytes 114720 | tf_op jit(solution)/shard_map/ppermute | solution.py:190
  123.1 1.7 convolution_bitcast_fusion.1
  124.8 14.1 %all_to_all.43 = f32[16,8,512]{2,1,0:T(8,128)} all-to-all(f32[16,8,512]{2,1,0:T(8,128)S(1)} %convolution_bitcast_fusion.1), channel_id=1, replica_groups=mesh['z'=8,'c'=2,'y'=4,'x'=4] {'y','x'}, dimensions={0} | all-to-all | bytes 524288 | tf_op jit(solution)/shard_map/all_to_all | solution.py:125
  138.9 1.0 reduce_sum.38
  139.9 0.7 broadcast_in_dim.15
  140.6 5.7 %all-to-all-start.6 = ((f32[8,8,512]{2,1,0:T(8,128)}), f32[8,8,512]{2,1,0:T(8,128)S(1)}, u32[]{:S(2)}, u32[]{:S(2)}) async-start(f32[8,8,512]{2,1,0:T(8,128)} %broadcast_in_dim.15), calls=%async_computation.6 | async-start | bytes 262144 | tf_op jit(solution)/shard_map/all_to_all | solution.py:125
  146.3 0.0 collective-permute-done.2
  146.3 1.9 broadcast_select_fusion.2
  148.2 13.4 %shard_map.67.in_ref = f32[512,512]{1,0:T(8,128)} custom-call(f32[256,384]{1,0:T(8,128)} %get-tuple-element.46.first_ref, f32[256,384]{1,0:T(8,128)} %get-tuple-element.45.second_ref), custom_call_target="tpu_custom_call" | custom-call | flops 6000000000 | bytes 2000000 | tf_op jit(solution)/shard_map/pallas_call | solution.py:113
  161.7 12.7 %shard_map.68 = f32[512,512]{1,0:T(8,128)} custom-call(f32[512,512]{1,0:T(8,128)} %shard_map.67.in_ref), custom_call_target="tpu_custom_call" | custom-call | flops 6000000000 | bytes 2000000 | tf_op jit(solution)/shard_map/pallas_call | solution.py:113
  174.4 0.0 all-to-all-done.6
  174.4 1.8 convolution_convert_fusion.1
  176.3 0.1 broadcast_in_dim.16
  176.4 18.8 %all_to_all.44 = bf16[16,64,512]{2,1,0:T(8,128)(2,1)} all-to-all(bf16[16,64,512]{2,1,0:T(8,128)(2,1)S(1)} %broadcast_in_dim.16), channel_id=1, replica_groups=mesh['z'=8,'c'=2,'y'=4,'x'=4] {'y','x'}, dimensions={0} | all-to-all | bytes 2097152 | tf_op jit(solution)/shard_map/all_to_all | solution.py:125
  195.1 2.7 %collective-permute-start.10 = (bf16[16,64,512]{2,1,0:T(8,128)(2,1)}, bf16[16,64,512]{2,1,0:T(8,128)(2,1)}, u32[]{:S(2)}, u32[]{:S(2)}) collective-permute-start(bf16[16,64,512]{2,1,0:T(8,128)(2,1)} %all_to_all.44), channel_id=1, source_target_pairs={{0,16},{16,0},{1,17},{17,1},{2,18},{18,2},{3,19},{19,3},{4,20},{20... | collective-permute-start | bytes 3145736 | tf_op jit(solution)/shard_map/ppermute | solution.py:134
  197.8 2.1 %convolution_convert_fusion = bf16[448,512]{1,0:T(8,128)(2,1)S(1)} fusion(f32[512,512]{1,0:T(8,128)} %shard_map.68, f32[448,256]{1,0:T(8,128)S(1)} %get-tuple-element.43, f32[448,256]{1,0:T(8,128)S(1)} %get-tuple-element.44), kind=kOutput, calls=%fused_computation.11 | convolution fusion | flops 705101824 | bytes 2424832 | tf_op jit(solution)/shard_map/dot_general | solution.py:69
  200.0 0.5 collective-permute-done.10
  200.5 1.7 select_bitcast_fusion.1
  202.2 0.2 maximum_bitcast_fusion
  202.4 0.6 multiply_reduce_fusion
  202.9 0.2 copy.9
  203.2 1.8 copy-done.1
  205.0 3.0 %fusion = f32[1,448,2048]{2,1,0:T(8,128)} fusion(bf16[448,512]{1,0:T(8,128)(2,1)S(1)} %convolution_convert_fusion, bf16[2048,512]{1,0:T(8,128)(2,1)S(1)} %bitcast.46, f32[1,448,2048]{2,1,0:T(8,128)S(1)} %copy-done.1, bf16[1,448,2048]{2,1,0:T(8,128)(2,1)S(1)} %copy-done.2), kind=kOutput, calls=%fused_computation.4 | convolution fusion | flops 943194112 | bytes 11730944 | tf_op jit(solution)/shard_map/dot_general | solution.py:212
  208.0 2.4 %subtract_convert_fusion = bf16[448,2048]{1,0:T(8,128)(2,1)} fusion(bf16[448,2048]{1,0:T(8,128)(2,1)S(1)} %copy-done.5, bf16[448,512]{1,0:T(8,128)(2,1)S(1)} %convolution_convert_fusion, bf16[2048,512]{1,0:T(8,128)(2,1)S(1)} %bitcast.47, f32[512]{0:T(512)S(1)} %add_sqrt_fusion), kind=kOutput, calls=%fused_computation.5 | convolution fusion | flops 946339840 | bytes 6227968 | tf_op jit(solution)/shard_map/dot_general | solution.py:213
  210.4 0.7 convert_divide_fusion
  (14 shorter events, 0.2 us)
Async XLA Ops:
  0.6 7.7 %copy-start = (f32[128,512]{1,0:T(8,128)S(1)}, f32[128,512]{1,0:T(8,128)}, u32[]{:S(2)}) copy-start(f32[128,512]{1,0:T(8,128)} %param.7) | copy-start | bytes 786436
  5.1 24.7 %copy-start.2 = (bf16[1,448,2048]{2,1,0:T(8,128)(2,1)S(1)}, bf16[1,448,2048]{2,1,0:T(8,128)(2,1)}, u32[]{:S(2)}) copy-start(bf16[1,448,2048]{2,1,0:T(8,128)(2,1)} %param.6) | copy-start | bytes 5505028
  5.1 27.4 %collective-permute-start = (bf16[448,2048]{1,0:T(8,128)(2,1)}, bf16[448,2048]{1,0:T(8,128)(2,1)}, u32[]{:S(2)}, u32[]{:S(2)}) collective-permute-start(bf16[448,2048]{1,0:T(8,128)(2,1)} %bitcast_convert_fusion), channel_id=1, source_target_pairs={{0,16},{16,0},{1,17},{17,1},{2,18},{18,2},{3,19},{19,3},{4,20},{20... | collective-permute-start | bytes 5505032 | tf_op jit(solution)/shard_map/ppermute | solution.py:134
  66.3 6.3 %collective-permute-start.1 = (f32[448,256]{1,0:T(8,128)S(1)}, f32[448,256]{1,0:T(8,128)}, u32[]{:S(2)}, u32[]{:S(2)}) collective-permute-start(f32[448,256]{1,0:T(8,128)S(1)} %bitcast.49), channel_id=1, source_target_pairs={{0,16},{16,0},{1,17},{17,1},{2,18},{18,2},{3,19},{19,3},{4,20},{20... | collective-permute-start | bytes 1376264 | tf_op jit(solution)/shard_map/ppermute | solution.py:134
  75.4 13.5 %all-to-all-start.3 = ((f32[16,16,384]{2,1,0:T(8,128)}), f32[16,16,384]{2,1,0:T(8,128)S(1)}, u32[]{:S(2)}, u32[]{:S(2)}) async-start(f32[16,16,384]{2,1,0:T(8,128)} %bitcast.52), calls=%async_computation.3 | async-start | bytes 786432 | tf_op jit(solution)/shard_map/all_to_all | solution.py:125
  89.7 25.0 %all-to-all-start.4 = ((f32[16,16,384]{2,1,0:T(8,128)}), f32[16,16,384]{2,1,0:T(8,128)S(1)}, u32[]{:S(2)}, u32[]{:S(2)}) async-start(f32[16,16,384]{2,1,0:T(8,128)} %broadcast_in_dim.14), calls=%async_computation.4 | async-start | bytes 786432 | tf_op jit(solution)/shard_map/all_to_all | solution.py:125
  95.9 6.7 %collective-permute-start.3 = (bf16[448,128]{1,0:T(8,128)(2,1)S(1)}, bf16[448,128]{1,0:T(8,128)(2,1)S(1)}, u32[]{:S(2)}, u32[]{:S(2)}) collective-permute-start(bf16[448,128]{1,0:T(8,128)(2,1)S(1)} %get-tuple-element.18), channel_id=1, source_target_pairs={{0,32},{32,64},{64,96},{96,128},{128,160},{160,192},{192,224},{224... | collective-permute-start | bytes 344072 | tf_op jit(solution)/shard_map/ppermute | solution.py:190
  96.2 9.2 %collective-permute-start.4 = (bf16[448,128]{1,0:T(8,128)(2,1)S(1)}, bf16[448,128]{1,0:T(8,128)(2,1)S(1)}, u32[]{:S(2)}, u32[]{:S(2)}) collective-permute-start(bf16[448,128]{1,0:T(8,128)(2,1)S(1)} %get-tuple-element.19), channel_id=1, source_target_pairs={{0,64},{32,96},{64,128},{96,160},{128,192},{160,224},{192,0},{224,... | collective-permute-start | bytes 344072 | tf_op jit(solution)/shard_map/ppermute | solution.py:190
  96.2 18.5 %collective-permute-start.5 = (bf16[448,128]{1,0:T(8,128)(2,1)S(1)}, bf16[448,128]{1,0:T(8,128)(2,1)}, u32[]{:S(2)}, u32[]{:S(2)}) collective-permute-start(bf16[448,128]{1,0:T(8,128)(2,1)S(1)} %get-tuple-element.20), channel_id=1, source_target_pairs={{0,96},{32,128},{64,160},{96,192},{128,224},{160,0},{192,32},{224,... | collective-permute-start | bytes 344072 | tf_op jit(solution)/shard_map/ppermute | solution.py:190
  98.3 18.4 %collective-permute-start.6 = (bf16[448,128]{1,0:T(8,128)(2,1)}, bf16[448,128]{1,0:T(8,128)(2,1)}, u32[]{:S(2)}, u32[]{:S(2)}) collective-permute-start(bf16[448,128]{1,0:T(8,128)(2,1)} %get-tuple-element.21), channel_id=1, source_target_pairs={{0,128},{32,160},{64,192},{96,224},{128,0},{160,32},{192,64},{224,... | collective-permute-start | bytes 344072 | tf_op jit(solution)/shard_map/ppermute | solution.py:190
  101.6 15.1 %collective-permute-start.7 = (bf16[448,128]{1,0:T(8,128)(2,1)}, bf16[448,128]{1,0:T(8,128)(2,1)}, u32[]{:S(2)}, u32[]{:S(2)}) collective-permute-start(bf16[448,128]{1,0:T(8,128)(2,1)} %get-tuple-element.22), channel_id=1, source_target_pairs={{0,160},{32,192},{64,224},{96,0},{128,32},{160,64},{192,96},{224,1... | collective-permute-start | bytes 344072 | tf_op jit(solution)/shard_map/ppermute | solution.py:190
  102.6 4.2 %copy-start.3 = (bf16[448,128]{1,0:T(8,128)(2,1)}, bf16[448,128]{1,0:T(8,128)(2,1)S(1)}, u32[]{:S(2)}) copy-start(bf16[448,128]{1,0:T(8,128)(2,1)S(1)} %collective-permute-done.3) | copy-start | bytes 344068
  102.6 17.6 %collective-permute-start.8 = (bf16[448,128]{1,0:T(8,128)(2,1)}, bf16[448,128]{1,0:T(8,128)(2,1)}, u32[]{:S(2)}, u32[]{:S(2)}) collective-permute-start(bf16[448,128]{1,0:T(8,128)(2,1)} %get-tuple-element.23), channel_id=1, source_target_pairs={{0,192},{32,224},{64,0},{96,32},{128,64},{160,96},{192,128},{224,1... | collective-permute-start | bytes 344072 | tf_op jit(solution)/shard_map/ppermute | solution.py:190
  105.4 1.4 copy-start.4
  105.4 17.7 %collective-permute-start.9 = (bf16[448,128]{1,0:T(8,128)(2,1)}, bf16[448,128]{1,0:T(8,128)(2,1)}, u32[]{:S(2)}, u32[]{:S(2)}) collective-permute-start(bf16[448,128]{1,0:T(8,128)(2,1)} %get-tuple-element.24), channel_id=1, source_target_pairs={{0,224},{32,0},{64,32},{96,64},{128,96},{160,128},{192,160},{224,1... | collective-permute-start | bytes 344072 | tf_op jit(solution)/shard_map/ppermute | solution.py:190
  114.7 31.6 %collective-permute-start.2 = (f32[256,384]{1,0:T(8,128)S(1)}, f32[256,384]{1,0:T(8,128)}, u32[]{:S(2)}, u32[]{:S(2)}) collective-permute-start(f32[256,384]{1,0:T(8,128)S(1)} %bitcast.53), channel_id=1, source_target_pairs={{0,16},{16,0},{1,17},{17,1},{2,18},{18,2},{3,19},{19,3},{4,20},{20... | collective-permute-start | bytes 1179656 | tf_op jit(solution)/shard_map/ppermute | solution.py:134
  140.6 33.8 %all-to-all-start.6 = ((f32[8,8,512]{2,1,0:T(8,128)}), f32[8,8,512]{2,1,0:T(8,128)S(1)}, u32[]{:S(2)}, u32[]{:S(2)}) async-start(f32[8,8,512]{2,1,0:T(8,128)} %broadcast_in_dim.15), calls=%async_computation.6 | async-start | bytes 262144 | tf_op jit(solution)/shard_map/all_to_all | solution.py:125
  195.1 5.4 %collective-permute-start.10 = (bf16[16,64,512]{2,1,0:T(8,128)(2,1)}, bf16[16,64,512]{2,1,0:T(8,128)(2,1)}, u32[]{:S(2)}, u32[]{:S(2)}) collective-permute-start(bf16[16,64,512]{2,1,0:T(8,128)(2,1)} %all_to_all.44), channel_id=1, source_target_pairs={{0,16},{16,0},{1,17},{17,1},{2,18},{18,2},{3,19},{19,3},{4,20},{20... | collective-permute-start | bytes 3145736 | tf_op jit(solution)/shard_map/ppermute | solution.py:134
  202.9 2.0 copy-start.1
  205.0 3.0 %copy-start.5 = (bf16[448,2048]{1,0:T(8,128)(2,1)S(1)}, bf16[448,2048]{1,0:T(8,128)(2,1)}, u32[]{:S(2)}) copy-start(bf16[448,2048]{1,0:T(8,128)(2,1)} %param.4) | copy-start | bytes 5505028
where the time goes:
time: 212 us; the launch traced here: 211 us
  blocking collectives  85.8 us (40%)
  starting transfers between devices  36.9 us (17%)
  Pallas kernels  26.2 us (12%)
  waiting for transfers between devices  24.9 us (12%)
  matrix products  17.6 us (8%)
  other arithmetic  14.3 us (7%)
  local copies, waits for them, and re-layouts  4.63 us (2%)
    all_to_all x5, blocking collectives, exchange(): return lax.all_to_all(value, axes, 0, 0, tiled=True)  85.8 us
    pallas_call x2, Pallas kernels, half_factor(): pl.pallas_call(kernel, out_shape=jax.ShapeDtypeStruct((size, size), f32),...  26.2 us
    ppermute x7, waiting for transfers between devices, per_device(): lax.ppermute(term, 'z', [(n, (n + shift) % depth) for n in range(depth)])  14.3 us
    all_to_all x3, starting transfers between devices, exchange(): return lax.all_to_all(value, axes, 0, 0, tiled=True)  13.2 us
    ppermute x4, starting transfers between devices, partner(): return lax.ppermute(value, 'c', SWAP)  12.7 us
    ppermute x7, starting transfers between devices, per_device(): lax.ppermute(term, 'z', [(n, (n + shift) % depth) for n in range(depth)])  10.9 us
    all_to_all x3, waiting for transfers between devices, exchange(): return lax.all_to_all(value, axes, 0, 0, tiled=True)  9.52 us
    dot_general x5, matrix products, exact_dot(): lax.dot_general(a, b, dims, precision=precision, preferred_element_type=f32)  7.33 us
  transfers between devices with their start and end apart: 14, of which 6 were waited for; matrix products, arithmetic and copies ran while one was open for 7% of the time, Pallas kernels for 12%

commit v1 on v0

--- a/solution.py
+++ b/solution.py
@@ -121,6 +121,136 @@
     )(*operands)
 
 
+def tile_rows(ref, pair):
+    parts = []
+    for z in (0, 1):
+        part = ref[:, 2 * pair + z].astype(f32)
+        parts.append(part.reshape(-1, part.shape[-1]))
+    return jnp.concatenate(parts, 0)
+
+
+def outer(left, right):
+    return lax.dot_general(left, right, (((1,), (1,)), ((), ())), preferred_element_type=f32)
+
+
+def own_kernel(where_ref, part_ref, left_ref, momentum_ref, gradient_ref, out_ref):
+    right = tile_rows(part_ref, pl.program_id(0)).astype(bf16)
+    feedback = outer(left_ref[...], right)
+    combined = momentum_ref[...] + gradient_ref[...].astype(f32)
+    out_ref[...] = combined - momentum_keep * feedback
+
+
+def rest_kernel(
+    where_ref,
+    mine_ref,
+    theirs_ref,
+    left_ref,
+    momentum_ref,
+    gradient_ref,
+    weights_ref,
+    done_ref,
+    momentum_out,
+    weights_out,
+    right_out,
+    norm_ref,
+    right_ref,
+):
+    step = pl.program_id(0)
+    steps = pl.num_programs(0) // 2
+    depth = mine_ref.shape[1]
+
+    @pl.when(step == 0)
+    def _():
+        squares = jnp.zeros(norm_ref.shape, f32)
+        count = 0
+        for ref in (mine_ref, theirs_ref):
+            for z in range(depth):
+                squares = squares + jnp.sum(jnp.square(ref[:, z].astype(f32)), axis=0)
+            count += ref.shape[0] * depth * ref.shape[2]
+        total = jnp.sum(squares, axis=0, keepdims=True)
+        norm_ref[...] = jnp.broadcast_to(1.0 / jnp.sqrt(total / count + tiny), norm_ref.shape)
+        for ref, owner in ((mine_ref, where_ref[0]), (theirs_ref, 1 - where_ref[0])):
+
+            @pl.when(where_ref[1] // depth == owner)
+            def _():
+                value = ref[:, lax.rem(where_ref[1], depth)].astype(f32) * norm_ref[...][None]
+                right_out[...] = value.reshape(right_out.shape)
+
+    @pl.when(step < steps)
+    def _():
+        right = tile_rows(theirs_ref, step)
+        right_ref[...] = right
+        feedback = outer(left_ref[...], right.astype(bf16))
+        combined = momentum_ref[...] + gradient_ref[...].astype(f32)
+        momentum_out[...] = combined - momentum_keep * feedback
+
+    @pl.when(step >= steps)
+    def _():
+        right_ref[...] = tile_rows(mine_ref, step - steps)
+
+    scaled = (right_ref[...] * norm_ref[0:1, :]).astype(bf16)
+    update = outer(left_ref[...], scaled)
+    value = weights_ref[...].astype(f32) - (learn_rate * (M / N) ** 0.5) * update
+    weights_out[...] = value.astype(bf16)
+
+
+def final_specs(part, left, half, tile):
+    whole = pl.BlockSpec(part.shape, lambda j, w: (0, 0, 0, 0))
+    factor = pl.BlockSpec(left.shape, lambda j, w: (0, 0))
+    rows = left.shape[0]
+    own = pl.BlockSpec((rows, tile), lambda j, w: (0, w[0] * half + j))
+    rest = pl.BlockSpec((rows, tile), lambda j, w: (0, (1 - w[0]) * half + jnp.minimum(j, half - 1)))
+    both = pl.BlockSpec(
+        (rows, tile), lambda j, w: (0, jnp.where(j < half, (1 - w[0]) * half + j, w[0] * half + j - half))
+    )
+    return whole, factor, own, rest, both
+
+
+def finish_own(where, part, left, momentum, gradient):
+    tile = 256
+    half = momentum.shape[1] // tile // 2
+    whole, factor, own, _, _ = final_specs(part, left, half, tile)
+    return pl.pallas_call(
+        own_kernel,
+        out_shape=jax.ShapeDtypeStruct(momentum.shape, f32),
+        grid_spec=pltpu.PrefetchScalarGridSpec(
+            num_scalar_prefetch=1, grid=(half,), in_specs=[whole, factor, own, own], out_specs=own
+        ),
+        cost_estimate=pl.CostEstimate(
+            flops=1_000_000_000, bytes_accessed=6_000_000, transcendentals=0
+        ),
+        name="finish_own",
+    )(where, part, left, momentum, gradient)
+
+
+def finish_rest(where, mine, theirs, left, momentum, gradient, weights, done):
+    tile = 256
+    half = momentum.shape[1] // tile // 2
+    whole, factor, _, rest, both = final_specs(mine, left, half, tile)
+    rank = left.shape[1]
+    short = mine.shape[0] * mine.shape[2]
+    return pl.pallas_call(
+        rest_kernel,
+        out_shape=[
+            jax.ShapeDtypeStruct(momentum.shape, f32),
+            jax.ShapeDtypeStruct(weights.shape, bf16),
+            jax.ShapeDtypeStruct((short, rank), f32),
+        ],
+        grid_spec=pltpu.PrefetchScalarGridSpec(
+            num_scalar_prefetch=1,
+            grid=(2 * half,),
+            in_specs=[whole, whole, factor, rest, rest, both, pl.BlockSpec(memory_space=pl.ANY)],
+            out_specs=[rest, both, pl.BlockSpec((short, rank), lambda j, w: (0, 0))],
+            scratch_shapes=[pltpu.VMEM((8, rank), f32), pltpu.VMEM((tile, rank), f32)],
+        ),
+        input_output_aliases={7: 0},
+        cost_estimate=pl.CostEstimate(
+            flops=2_000_000_000, bytes_accessed=12_000_000, transcendentals=1000
+        ),
+        name="finish_rest",
+    )(where, mine, theirs, left, momentum, gradient, weights, done)
+
+
 def exchange(value, axes):
     return lax.all_to_all(value, axes, 0, 0, tiled=True)
 
@@ -157,9 +287,8 @@
     mine = combined.astype(bf16)
     theirs = partner(mine)
 
-    left = jnp.dot(mine, right_half, preferred_element_type=f32) + jnp.dot(
-        theirs, right_half, preferred_element_type=f32
-    )
+    pair = (mine.astype(f32) + theirs.astype(f32)).astype(bf16)
+    left = jnp.dot(pair, right_half, preferred_element_type=f32)
     left = exchange(left.astype(bf16).reshape(depth, rows // depth, half), "z")
     left = left.astype(f32).sum(0) / groups
     left = gather(left, "z").reshape(rows, half)
@@ -183,8 +312,7 @@
     terms = []
     for shift in range(depth):
         at = core * wide + lax.rem(place + shift, depth) * width
-        term = lax.dynamic_slice_in_dim(mine, at, width, 1).astype(f32)
-        term = (term + lax.dynamic_slice_in_dim(theirs, at, width, 1).astype(f32)).astype(bf16)
+        term = lax.dynamic_slice_in_dim(pair, at, width, 1)
         if shift > 0:
             term, _ = lax.optimization_barrier((term, left))
             term = lax.ppermute(term, "z", [(n, (n + shift) % depth) for n in range(depth)])
@@ -196,24 +324,17 @@
     crossed = crossed.sum(0)
     crossed = gather(crossed, "z").reshape(-1, rank)
 
-    turn = (((1,), (1,)), ((), ()))
     part = exact_dot(crossed, inverse, 1, 1, THREE)
     part = gather(part.astype(bf16), ROWS)
     left_half = exact_dot(left_mean, inverse, 1, 1, THREE).astype(bf16)
-    right_mean = jnp.stack(in_order(part, partner(part), core), 0)
-    right_mean = right_mean.reshape(2, blocks, depth, -1, rank)
-    right_mean = jnp.moveaxis(right_mean, 2, 1).reshape(columns, rank)
-
-    squares = jnp.sum(jnp.square(right_mean.astype(f32)), axis=0)
-    norm = jnp.sqrt(squares / columns + tiny)
-    short = columns // blocks
-    new_right = lax.dynamic_slice_in_dim(right_mean, me * short, short, 0).astype(f32) / norm
-    scaled = (right_mean.astype(f32) / norm).astype(bf16)
-    feedback = lax.dot_general(left_half, right_mean, turn, preferred_element_type=f32)
-    update = lax.dot_general(left_half, scaled, turn, preferred_element_type=f32)
-    new_momentum = combined - momentum_keep * feedback
-    new_weights = (weights.astype(f32) - learn_rate * jnp.sqrt(M / N) * update).astype(bf16)
-    return (new_weights, new_momentum[None], new_right)
+    part = part.reshape(blocks, depth, -1, rank)
+    other = partner(part)
+    where = jnp.where(jnp.arange(2) == 0, core, me).astype(jnp.int32)
+    moved = finish_own(where, part, left_half, momentum[0], gradient[0])
+    moved, new_weights, new_right = finish_rest(
+        where, part, other, left_half, momentum[0], gradient[0], weights, moved
+    )
+    return (new_weights, moved[None], new_right)
 
 
 def solution(mesh):

time: 212 us -> 210 us (level)
  blocking collectives: 85.8 us -> 63.5 us
  Pallas kernels: 26.2 us -> 41.6 us
  waiting for transfers between devices: 24.9 us -> 38.1 us
  matrix products: 17.6 us -> 8.1 us
  starting transfers between devices: 36.9 us -> 43.6 us
  other arithmetic: 14.3 us -> 8.26 us
    all_to_all x5 -> x4, blocking collectives: 85.8 us -> 63.5 us  [exchange(): return lax.all_to_all(value, axes, 0, 0, tiled=True)]
    pallas_call x0 -> x2, Pallas kernels: none -> 15.4 us  [the longest x1 9.85 us: finish_rest(): pl.pallas_call(rest_kernel, out_shape=[jax.ShapeDtypeStruct(momentum.shap...]
    all_to_all x3 -> x4, waiting for transfers between devices: 9.52 us -> 23.4 us  [exchange(): return lax.all_to_all(value, axes, 0, 0, tiled=True)]
    dot_general x4 -> x1, matrix products: 10.3 us -> 2.42 us  [per_device(): left = jnp.dot(pair, right_half, preferred_element_type=f32)]
    all_to_all x3 -> x4, starting transfers between devices: 13.2 us -> 19.6 us  [exchange(): return lax.all_to_all(value, axes, 0, 0, tiled=True)]
  transfers between devices with their start and end apart: 14 -> 15, of which waited for: 6 -> 6; matrix products, arithmetic and copies ran while one was open for 7% -> 5% of each run, Pallas kernels for 12% -> 15%
where the time goes in v1:
time: 210 us; the launch traced here: 209 us
  blocking collectives  63.5 us (30%)
  starting transfers between devices  43.6 us (21%)
  Pallas kernels  41.6 us (20%)
  waiting for transfers between devices  38.1 us (18%)
  other arithmetic  8.26 us (4%)
  matrix products  8.1 us (4%)
  local copies, waits for them, and re-layouts  4.55 us (2%)
    all_to_all x4, blocking collectives, exchange(): return lax.all_to_all(value, axes, 0, 0, tiled=True)  63.5 us
    pallas_call x2, Pallas kernels, half_factor(): pl.pallas_call(kernel, out_shape=jax.ShapeDtypeStruct((size, size), f32),...  26.2 us
    all_to_all x4, waiting for transfers between devices, exchange(): return lax.all_to_all(value, axes, 0, 0, tiled=True)  23.4 us
    all_to_all x4, starting transfers between devices, exchange(): return lax.all_to_all(value, axes, 0, 0, tiled=True)  19.6 us
    ppermute x7, waiting for transfers between devices, per_device(): lax.ppermute(term, 'z', [(n, (n + shift) % depth) for n in range(depth)])  14.3 us
    ppermute x4, starting transfers between devices, partner(): return lax.ppermute(value, 'c', SWAP)  13 us
    ppermute x7, starting transfers between devices, per_device(): lax.ppermute(term, 'z', [(n, (n + shift) % depth) for n in range(depth)])  11 us
    pallas_call x1, Pallas kernels, finish_rest(): pl.pallas_call(rest_kernel, out_shape=[jax.ShapeDtypeStruct(momentum.shap...  9.85 us
  transfers between devices with their start and end apart: 15, of which 6 were waited for; matrix products, arithmetic and copies ran while one was open for 5% of the time, Pallas kernels for 15%

profile of v1, /device:TPU:1, one launch (start us, length us, event | category | flops | bytes accessed | tf_op | source)
XLA Modules:
  0.0 208.6 jit_solution(13143287173895189113)
XLA Ops:
  0.6 0.0 copy-start
  0.6 3.2 %add_convert_fusion.1 = bf16[448,2048]{1,0:T(8,128)(2,1)S(1)} fusion(bf16[1,448,2048]{2,1,0:T(8,128)(2,1)} %param.6, f32[1,448,2048]{2,1,0:T(8,128)} %param.5), kind=kLoop, calls=%fused_computation.1 | loop fusion | flops 2752512 | bytes 7340032 | tf_op jit(solution)/shard_map/convert_element_type | solution.py:287
  3.9 3.3 %collective-permute-start = (bf16[448,2048]{1,0:T(8,128)(2,1)S(1)}, bf16[448,2048]{1,0:T(8,128)(2,1)}, u32[]{:S(2)}, u32[]{:S(2)}) collective-permute-start(bf16[448,2048]{1,0:T(8,128)(2,1)S(1)} %add_convert_fusion.1), channel_id=1, source_target_pairs={{0,16},{16,0},{1,17},{17,1},{2,18},{18,2},{3,19},{19,3},{4,20},{20... | collective-permute-start | bytes 5505032 | tf_op jit(solution)/shard_map/ppermute | solution.py:264
  7.2 0.0 copy-done
  7.2 1.1 broadcast_in_dim.20
  8.2 5.1 %all-to-all-start = ((bf16[16,128,256]{2,1,0:T(8,128)(2,1)}), bf16[16,128,256]{2,1,0:T(8,128)(2,1)}, u32[]{:S(2)}, u32[]{:S(2)}) async-start(bf16[16,128,256]{2,1,0:T(8,128)(2,1)} %broadcast_in_dim.20), calls=%async_computation | async-start | bytes 2097152 | tf_op jit(solution)/shard_map/all_to_all | solution.py:255
  13.4 0.0 collective-permute-done
  13.4 3.4 %add_convert_fusion = bf16[448,2048]{1,0:T(8,128)(2,1)} fusion(bf16[448,2048]{1,0:T(8,128)(2,1)} %collective-permute-done, bf16[448,2048]{1,0:T(8,128)(2,1)S(1)} %add_convert_fusion.1), kind=kLoop, calls=%fused_computation | loop fusion | flops 3670016 | bytes 5505024 | tf_op jit(solution)/shard_map/convert_element_type | solution.py:290
  16.8 13.9 %all-to-all-done = bf16[16,128,256]{2,1,0:T(8,128)(2,1)} async-done(((bf16[16,128,256]{2,1,0:T(8,128)(2,1)}), bf16[16,128,256]{2,1,0:T(8,128)(2,1)}, u32[]{:S(2)}, u32[]{:S(2)}) %all-to-all-start) | async-done | bytes 1048608 | tf_op jit(solution)/shard_map/all_to_all | solution.py:255
  30.6 2.4 %convolution_convert_fusion.1 = bf16[448,256]{1,0:T(8,128)(2,1)S(1)} fusion(bf16[448,2048]{1,0:T(8,128)(2,1)} %add_convert_fusion, bf16[2048,256]{1,0:T(8,128)(2,1)} %bitcast.2), kind=kOutput, calls=%fused_computation.3 | convolution fusion | flops 469876736 | bytes 3112960 | tf_op jit(solution)/shard_map/dot_general | solution.py:291
  33.0 16.9 %all_to_all.40 = bf16[8,56,256]{2,1,0:T(8,128)(2,1)S(1)} all-to-all(bf16[8,56,256]{2,1,0:T(8,128)(2,1)S(1)} %bitcast.40), channel_id=1, replica_groups=mesh['z'=8,'c'=2,'y'=4,'x'=4] {'z'}, dimensions={0} | all-to-all | bytes 458752 | tf_op jit(solution)/shard_map/all_to_all | solution.py:255
  50.0 14.7 %all_to_all.41 = f32[8,56,256]{2,1,0:T(8,128)S(1)} all-to-all(f32[8,56,256]{2,1,0:T(8,128)S(1)} %broadcast_in_dim.21), channel_id=1, replica_groups=mesh['z'=8,'c'=2,'y'=4,'x'=4] {'z'}, dimensions={0} | all-to-all | bytes 917504 | tf_op jit(solution)/shard_map/all_to_all | solution.py:255
  64.7 4.8 %collective-permute-start.8 = (f32[448,256]{1,0:T(8,128)S(1)}, f32[448,256]{1,0:T(8,128)S(1)}, u32[]{:S(2)}, u32[]{:S(2)}) collective-permute-start(f32[448,256]{1,0:T(8,128)S(1)} %bitcast.37), channel_id=1, source_target_pairs={{0,16},{16,0},{1,17},{17,1},{2,18},{18,2},{3,19},{19,3},{4,20},{20... | collective-permute-start | bytes 1376264 | tf_op jit(solution)/shard_map/ppermute | solution.py:264
  69.4 1.0 convolution_bitcast_fusion
  70.4 0.4 collective-permute-done.8
  70.9 0.1 broadcast_select_fusion
  70.9 0.6 fusion.16
  71.6 0.0 copy-start.3
  71.6 0.9 copy.8
  72.6 5.1 %all-to-all-start.3 = ((f32[16,16,384]{2,1,0:T(8,128)}), f32[16,16,384]{2,1,0:T(8,128)S(1)}, u32[]{:S(2)}, u32[]{:S(2)}) async-start(f32[16,16,384]{2,1,0:T(8,128)} %bitcast.38), calls=%async_computation.3 | async-start | bytes 786432 | tf_op jit(solution)/shard_map/all_to_all | solution.py:255
  77.7 9.5 %all-to-all-done.3 = f32[16,16,384]{2,1,0:T(8,128)S(1)} async-done(((f32[16,16,384]{2,1,0:T(8,128)}), f32[16,16,384]{2,1,0:T(8,128)S(1)}, u32[]{:S(2)}, u32[]{:S(2)}) %all-to-all-start.3) | async-done | bytes 393248 | tf_op jit(solution)/shard_map/all_to_all | solution.py:255
  87.3 0.8 broadcast_in_dim.24
  88.0 3.6 %all-to-all-start.4 = ((f32[16,16,384]{2,1,0:T(8,128)}), f32[16,16,384]{2,1,0:T(8,128)S(1)}, u32[]{:S(2)}, u32[]{:S(2)}) async-start(f32[16,16,384]{2,1,0:T(8,128)} %broadcast_in_dim.24), calls=%async_computation.4 | async-start | bytes 786432 | tf_op jit(solution)/shard_map/all_to_all | solution.py:255
  91.7 0.0 copy-done.3
  91.7 1.0 constant_dynamic-slice_fusion
  92.6 0.3 collective-permute-start.1
  92.9 0.1 collective-permute-start.2
  93.0 2.0 collective-permute-start.3
  95.0 3.3 %collective-permute-start.4 = (bf16[448,128]{1,0:T(8,128)(2,1)}, bf16[448,128]{1,0:T(8,128)(2,1)S(1)}, u32[]{:S(2)}, u32[]{:S(2)}) collective-permute-start(bf16[448,128]{1,0:T(8,128)(2,1)} %get-tuple-element.24), channel_id=1, source_target_pairs={{0,128},{32,160},{64,192},{96,224},{128,0},{160,32},{192,64},{224,... | collective-permute-start | bytes 344072 | tf_op jit(solution)/shard_map/ppermute | solution.py:318
  98.3 0.9 collective-permute-start.5
  99.2 0.0 collective-permute-done.1
  99.2 2.9 %collective-permute-start.6 = (bf16[448,128]{1,0:T(8,128)(2,1)}, bf16[448,128]{1,0:T(8,128)(2,1)S(1)}, u32[]{:S(2)}, u32[]{:S(2)}) collective-permute-start(bf16[448,128]{1,0:T(8,128)(2,1)} %get-tuple-element.26), channel_id=1, source_target_pairs={{0,192},{32,224},{64,0},{96,32},{128,64},{160,96},{192,128},{224,1... | collective-permute-start | bytes 344072 | tf_op jit(solution)/shard_map/ppermute | solution.py:318
  102.1 0.0 collective-permute-done.2
  102.2 1.5 collective-permute-start.7
  103.7 7.7 %collective-permute-done.3 = bf16[448,128]{1,0:T(8,128)(2,1)S(1)} collective-permute-done((bf16[448,128]{1,0:T(8,128)(2,1)S(1)}, bf16[448,128]{1,0:T(8,128)(2,1)S(1)}, u32[]{:S(2)}, u32[]{:S(2)}) %collective-permute-start.3) | collective-permute-done | bytes 114720 | tf_op jit(solution)/shard_map/ppermute | solution.py:318
  111.4 0.0 all-to-all-done.4
  111.4 2.0 collective-permute-start.9
  113.4 0.0 collective-permute-done.4
  113.4 0.0 collective-permute-done.5
  113.4 3.1 %collective-permute-done.6 = bf16[448,128]{1,0:T(8,128)(2,1)S(1)} collective-permute-done((bf16[448,128]{1,0:T(8,128)(2,1)}, bf16[448,128]{1,0:T(8,128)(2,1)S(1)}, u32[]{:S(2)}, u32[]{:S(2)}) %collective-permute-start.6) | collective-permute-done | bytes 114720 | tf_op jit(solution)/shard_map/ppermute | solution.py:318
  116.4 3.5 %collective-permute-done.7 = bf16[448,128]{1,0:T(8,128)(2,1)S(1)} collective-permute-done((bf16[448,128]{1,0:T(8,128)(2,1)}, bf16[448,128]{1,0:T(8,128)(2,1)S(1)}, u32[]{:S(2)}, u32[]{:S(2)}) %collective-permute-start.7) | collective-permute-done | bytes 114720 | tf_op jit(solution)/shard_map/ppermute | solution.py:318
  119.9 0.5 convolution_bitcast_fusion.1
  120.4 13.8 %all_to_all.42 = f32[16,8,512]{2,1,0:T(8,128)S(1)} all-to-all(f32[16,8,512]{2,1,0:T(8,128)S(1)} %convolution_bitcast_fusion.1), channel_id=1, replica_groups=mesh['z'=8,'c'=2,'y'=4,'x'=4] {'y','x'}, dimensions={0} | all-to-all | bytes 524288 | tf_op jit(solution)/shard_map/all_to_all | solution.py:255
  134.3 0.7 broadcast_in_dim.46
  134.9 5.8 %all-to-all-start.6 = ((f32[8,8,512]{2,1,0:T(8,128)}), f32[8,8,512]{2,1,0:T(8,128)S(1)}, u32[]{:S(2)}, u32[]{:S(2)}) async-start(f32[8,8,512]{2,1,0:T(8,128)} %broadcast_in_dim.46), calls=%async_computation.6 | async-start | bytes 262144 | tf_op jit(solution)/shard_map/all_to_all | solution.py:255
  140.7 0.0 collective-permute-done.9
  140.8 0.9 broadcast_select_fusion.2
  141.7 13.4 %shard_map.67.in_ref = f32[512,512]{1,0:T(8,128)} custom-call(f32[256,384]{1,0:T(8,128)} %get-tuple-element.50.first_ref, f32[256,384]{1,0:T(8,128)} %get-tuple-element.49.second_ref), custom_call_target="tpu_custom_call" | custom-call | flops 6000000000 | bytes 2000000 | tf_op jit(solution)/shard_map/pallas_call | solution.py:113
  155.1 12.7 %shard_map.68 = f32[512,512]{1,0:T(8,128)} custom-call(f32[512,512]{1,0:T(8,128)} %shard_map.67.in_ref), custom_call_target="tpu_custom_call" | custom-call | flops 6000000000 | bytes 2000000 | tf_op jit(solution)/shard_map/pallas_call | solution.py:113
  167.9 0.0 all-to-all-done.6
  167.9 1.8 convolution_convert_fusion.2
  169.7 0.0 copy-start.2
  169.7 0.1 broadcast_in_dim.47
  169.8 18.2 %all_to_all.43 = bf16[16,64,512]{2,1,0:T(8,128)(2,1)S(1)} all-to-all(bf16[16,64,512]{2,1,0:T(8,128)(2,1)S(1)} %broadcast_in_dim.47), channel_id=1, replica_groups=mesh['z'=8,'c'=2,'y'=4,'x'=4] {'y','x'}, dimensions={0} | all-to-all | bytes 2097152 | tf_op jit(solution)/shard_map/all_to_all | solution.py:255
  188.0 0.0 copy-start.1
  188.0 3.0 %collective-permute-start.10 = (bf16[16,8,8,512]{3,2,1,0:T(8,128)(2,1)S(1)}, bf16[16,8,8,512]{3,2,1,0:T(8,128)(2,1)}, u32[]{:S(2)}, u32[]{:S(2)}) collective-permute-start(bf16[16,8,8,512]{3,2,1,0:T(8,128)(2,1)S(1)} %bitcast.34), channel_id=1, source_target_pairs={{0,16},{16,0},{1,17},{17,1},{2,18},{18,2},{3,19},{19,3},{4,20},{20... | collective-permute-start | bytes 3145736 | tf_op jit(solution)/shard_map/ppermute | solution.py:264
  190.9 0.5 compare_select_fusion.where_ref
  191.5 0.0 copy-done.2
  191.5 1.7 convolution_convert_fusion.left_ref
  193.2 0.0 copy-done.1
  193.2 5.6 %finish_own.1.done_ref = f32[448,2048]{1,0:T(8,128)} custom-call(s32[2]{0:T(128)} %compare_select_fusion.where_ref, bf16[16,8,8,512]{3,2,1,0:T(8,128)(2,1)} %bitcast.35, bf16[448,512]{1,0:T(8,128)(2,1)} %convolution_convert_fusion.left_ref, f32[448,2048]{1,0:T(8,128)} %bitcast.29, bf16[448,2048]{1,0:T(8,128)(2,1)} %bitcast.31), custom_call_target="tpu_custom_call" | custom-call | flops 1000000000 | bytes 6000000 | tf_op jit(solution)/shard_map/finish_own/pallas_call | solution.py:213
  198.8 0.0 collective-permute-done.10.theirs_ref
  198.8 9.8 %finish_rest.1 = (f32[448,2048]{1,0:T(8,128)}, bf16[448,2048]{1,0:T(8,128)(2,1)}, f32[128,512]{1,0:T(8,128)}) custom-call(s32[2]{0:T(128)} %compare_select_fusion.where_ref, bf16[16,8,8,512]{3,2,1,0:T(8,128)(2,1)} %bitcast.36, bf16[16,8,8,512]{3,2,1,0:T(8,128)(2,1)} %collective-permute-done.10.theirs_ref, ...), custom_call_target="tpu_custom_call", output_to_operand_aliasing={{0}: (7, {})} | custom-call | flops 2000000000 | bytes 12000000 | tf_op jit(solution)/shard_map/finish_rest/pallas_call | solution.py:232
  (7 shorter events, 0.2 us)
Async XLA Ops:
  0.6 6.5 %copy-start = (f32[128,512]{1,0:T(8,128)S(1)}, f32[128,512]{1,0:T(8,128)}, u32[]{:S(2)}) copy-start(f32[128,512]{1,0:T(8,128)} %param.7) | copy-start | bytes 786436
  3.9 9.5 %collective-permute-start = (bf16[448,2048]{1,0:T(8,128)(2,1)S(1)}, bf16[448,2048]{1,0:T(8,128)(2,1)}, u32[]{:S(2)}, u32[]{:S(2)}) collective-permute-start(bf16[448,2048]{1,0:T(8,128)(2,1)S(1)} %add_convert_fusion.1), channel_id=1, source_target_pairs={{0,16},{16,0},{1,17},{17,1},{2,18},{18,2},{3,19},{19,3},{4,20},{20... | collective-permute-start | bytes 5505032 | tf_op jit(solution)/shard_map/ppermute | solution.py:264
  8.2 22.4 %all-to-all-start = ((bf16[16,128,256]{2,1,0:T(8,128)(2,1)}), bf16[16,128,256]{2,1,0:T(8,128)(2,1)}, u32[]{:S(2)}, u32[]{:S(2)}) async-start(bf16[16,128,256]{2,1,0:T(8,128)(2,1)} %broadcast_in_dim.20), calls=%async_computation | async-start | bytes 2097152 | tf_op jit(solution)/shard_map/all_to_all | solution.py:255
  64.7 6.2 %collective-permute-start.8 = (f32[448,256]{1,0:T(8,128)S(1)}, f32[448,256]{1,0:T(8,128)S(1)}, u32[]{:S(2)}, u32[]{:S(2)}) collective-permute-start(f32[448,256]{1,0:T(8,128)S(1)} %bitcast.37), channel_id=1, source_target_pairs={{0,16},{16,0},{1,17},{17,1},{2,18},{18,2},{3,19},{19,3},{4,20},{20... | collective-permute-start | bytes 1376264 | tf_op jit(solution)/shard_map/ppermute | solution.py:264
  71.6 20.0 %copy-start.3 = (bf16[448,2048]{1,0:T(8,128)(2,1)S(1)}, bf16[448,2048]{1,0:T(8,128)(2,1)}, u32[]{:S(2)}) copy-start(bf16[448,2048]{1,0:T(8,128)(2,1)} %add_convert_fusion) | copy-start | bytes 5505028
  72.6 14.7 %all-to-all-start.3 = ((f32[16,16,384]{2,1,0:T(8,128)}), f32[16,16,384]{2,1,0:T(8,128)S(1)}, u32[]{:S(2)}, u32[]{:S(2)}) async-start(f32[16,16,384]{2,1,0:T(8,128)} %bitcast.38), calls=%async_computation.3 | async-start | bytes 786432 | tf_op jit(solution)/shard_map/all_to_all | solution.py:255
  88.0 23.3 %all-to-all-start.4 = ((f32[16,16,384]{2,1,0:T(8,128)}), f32[16,16,384]{2,1,0:T(8,128)S(1)}, u32[]{:S(2)}, u32[]{:S(2)}) async-start(f32[16,16,384]{2,1,0:T(8,128)} %broadcast_in_dim.24), calls=%async_computation.4 | async-start | bytes 786432 | tf_op jit(solution)/shard_map/all_to_all | solution.py:255
  92.6 6.6 %collective-permute-start.1 = (bf16[448,128]{1,0:T(8,128)(2,1)S(1)}, bf16[448,128]{1,0:T(8,128)(2,1)S(1)}, u32[]{:S(2)}, u32[]{:S(2)}) collective-permute-start(bf16[448,128]{1,0:T(8,128)(2,1)S(1)} %get-tuple-element.21), channel_id=1, source_target_pairs={{0,32},{32,64},{64,96},{96,128},{128,160},{160,192},{192,224},{224... | collective-permute-start | bytes 344072 | tf_op jit(solution)/shard_map/ppermute | solution.py:318
  92.9 9.2 %collective-permute-start.2 = (bf16[448,128]{1,0:T(8,128)(2,1)S(1)}, bf16[448,128]{1,0:T(8,128)(2,1)S(1)}, u32[]{:S(2)}, u32[]{:S(2)}) collective-permute-start(bf16[448,128]{1,0:T(8,128)(2,1)S(1)} %get-tuple-element.22), channel_id=1, source_target_pairs={{0,64},{32,96},{64,128},{96,160},{128,192},{160,224},{192,0},{224,... | collective-permute-start | bytes 344072 | tf_op jit(solution)/shard_map/ppermute | solution.py:318
  93.0 18.3 %collective-permute-start.3 = (bf16[448,128]{1,0:T(8,128)(2,1)S(1)}, bf16[448,128]{1,0:T(8,128)(2,1)S(1)}, u32[]{:S(2)}, u32[]{:S(2)}) collective-permute-start(bf16[448,128]{1,0:T(8,128)(2,1)S(1)} %get-tuple-element.23), channel_id=1, source_target_pairs={{0,96},{32,128},{64,160},{96,192},{128,224},{160,0},{192,32},{224,... | collective-permute-start | bytes 344072 | tf_op jit(solution)/shard_map/ppermute | solution.py:318
  95.0 18.3 %collective-permute-start.4 = (bf16[448,128]{1,0:T(8,128)(2,1)}, bf16[448,128]{1,0:T(8,128)(2,1)S(1)}, u32[]{:S(2)}, u32[]{:S(2)}) collective-permute-start(bf16[448,128]{1,0:T(8,128)(2,1)} %get-tuple-element.24), channel_id=1, source_target_pairs={{0,128},{32,160},{64,192},{96,224},{128,0},{160,32},{192,64},{224,... | collective-permute-start | bytes 344072 | tf_op jit(solution)/shard_map/ppermute | solution.py:318
  98.3 15.0 %collective-permute-start.5 = (bf16[448,128]{1,0:T(8,128)(2,1)}, bf16[448,128]{1,0:T(8,128)(2,1)S(1)}, u32[]{:S(2)}, u32[]{:S(2)}) collective-permute-start(bf16[448,128]{1,0:T(8,128)(2,1)} %get-tuple-element.25), channel_id=1, source_target_pairs={{0,160},{32,192},{64,224},{96,0},{128,32},{160,64},{192,96},{224,1... | collective-permute-start | bytes 344072 | tf_op jit(solution)/shard_map/ppermute | solution.py:318
  99.2 17.2 %collective-permute-start.6 = (bf16[448,128]{1,0:T(8,128)(2,1)}, bf16[448,128]{1,0:T(8,128)(2,1)S(1)}, u32[]{:S(2)}, u32[]{:S(2)}) collective-permute-start(bf16[448,128]{1,0:T(8,128)(2,1)} %get-tuple-element.26), channel_id=1, source_target_pairs={{0,192},{32,224},{64,0},{96,32},{128,64},{160,96},{192,128},{224,1... | collective-permute-start | bytes 344072 | tf_op jit(solution)/shard_map/ppermute | solution.py:318
  102.2 17.8 %collective-permute-start.7 = (bf16[448,128]{1,0:T(8,128)(2,1)}, bf16[448,128]{1,0:T(8,128)(2,1)S(1)}, u32[]{:S(2)}, u32[]{:S(2)}) collective-permute-start(bf16[448,128]{1,0:T(8,128)(2,1)} %get-tuple-element.27), channel_id=1, source_target_pairs={{0,224},{32,0},{64,32},{96,64},{128,96},{160,128},{192,160},{224,1... | collective-permute-start | bytes 344072 | tf_op jit(solution)/shard_map/ppermute | solution.py:318
  111.4 29.4 %collective-permute-start.9 = (f32[256,384]{1,0:T(8,128)S(1)}, f32[256,384]{1,0:T(8,128)S(1)}, u32[]{:S(2)}, u32[]{:S(2)}) collective-permute-start(f32[256,384]{1,0:T(8,128)S(1)} %bitcast.39), channel_id=1, source_target_pairs={{0,16},{16,0},{1,17},{17,1},{2,18},{18,2},{3,19},{19,3},{4,20},{20... | collective-permute-start | bytes 1179656 | tf_op jit(solution)/shard_map/ppermute | solution.py:264
  134.9 32.9 %all-to-all-start.6 = ((f32[8,8,512]{2,1,0:T(8,128)}), f32[8,8,512]{2,1,0:T(8,128)S(1)}, u32[]{:S(2)}, u32[]{:S(2)}) async-start(f32[8,8,512]{2,1,0:T(8,128)} %broadcast_in_dim.46), calls=%async_computation.6 | async-start | bytes 262144 | tf_op jit(solution)/shard_map/all_to_all | solution.py:255
  169.7 21.8 %copy-start.2 = (f32[512,512]{1,0:T(8,128)S(1)}, f32[512,512]{1,0:T(8,128)}, u32[]{:S(2)}) copy-start(f32[512,512]{1,0:T(8,128)} %shard_map.68) | copy-start | bytes 3145732
  188.0 5.2 %copy-start.1 = (bf16[16,64,512]{2,1,0:T(8,128)(2,1)}, bf16[16,64,512]{2,1,0:T(8,128)(2,1)S(1)}, u32[]{:S(2)}) copy-start(bf16[16,64,512]{2,1,0:T(8,128)(2,1)S(1)} %all_to_all.43) | copy-start | bytes 3145732
  188.0 10.8 %collective-permute-start.10 = (bf16[16,8,8,512]{3,2,1,0:T(8,128)(2,1)S(1)}, bf16[16,8,8,512]{3,2,1,0:T(8,128)(2,1)}, u32[]{:S(2)}, u32[]{:S(2)}) collective-permute-start(bf16[16,8,8,512]{3,2,1,0:T(8,128)(2,1)S(1)} %bitcast.34), channel_id=1, source_target_pairs={{0,16},{16,0},{1,17},{17,1},{2,18},{18,2},{3,19},{19,3},{4,20},{20... | collective-permute-start | bytes 3145736 | tf_op jit(solution)/shard_map/ppermute | solution.py:264

commit v2 on v0

--- a/solution.py
+++ b/solution.py
@@ -118,6 +118,7 @@
         cost_estimate=pl.CostEstimate(
             flops=6_000_000_000, bytes_accessed=2_000_000, transcendentals=1000
         ),
+        compiler_params=pltpu.CompilerParams(vmem_limit_bytes=8 << 20),
     )(*operands)
 
 
@@ -157,9 +158,8 @@
     mine = combined.astype(bf16)
     theirs = partner(mine)
 
-    left = jnp.dot(mine, right_half, preferred_element_type=f32) + jnp.dot(
-        theirs, right_half, preferred_element_type=f32
-    )
+    pair = (mine.astype(f32) + theirs.astype(f32)).astype(bf16)
+    left = jnp.dot(pair, right_half, preferred_element_type=f32)
     left = exchange(left.astype(bf16).reshape(depth, rows // depth, half), "z")
     left = left.astype(f32).sum(0) / groups
     left = gather(left, "z").reshape(rows, half)
@@ -183,8 +183,7 @@
     terms = []
     for shift in range(depth):
         at = core * wide + lax.rem(place + shift, depth) * width
-        term = lax.dynamic_slice_in_dim(mine, at, width, 1).astype(f32)
-        term = (term + lax.dynamic_slice_in_dim(theirs, at, width, 1).astype(f32)).astype(bf16)
+        term = lax.dynamic_slice_in_dim(pair, at, width, 1)
         if shift > 0:
             term, _ = lax.optimization_barrier((term, left))
             term = lax.ppermute(term, "z", [(n, (n + shift) % depth) for n in range(depth)])
@@ -200,7 +199,8 @@
     part = exact_dot(crossed, inverse, 1, 1, THREE)
     part = gather(part.astype(bf16), ROWS)
     left_half = exact_dot(left_mean, inverse, 1, 1, THREE).astype(bf16)
-    right_mean = jnp.stack(in_order(part, partner(part), core), 0)
+    other = partner(part)
+    right_mean = jnp.stack(in_order(part, other, core), 0)
     right_mean = right_mean.reshape(2, blocks, depth, -1, rank)
     right_mean = jnp.moveaxis(right_mean, 2, 1).reshape(columns, rank)
 
@@ -209,9 +209,10 @@
     short = columns // blocks
     new_right = lax.dynamic_slice_in_dim(right_mean, me * short, short, 0).astype(f32) / norm
     scaled = (right_mean.astype(f32) / norm).astype(bf16)
+    turn = (((1,), (1,)), ((), ()))
     feedback = lax.dot_general(left_half, right_mean, turn, preferred_element_type=f32)
     update = lax.dot_general(left_half, scaled, turn, preferred_element_type=f32)
-    new_momentum = combined - momentum_keep * feedback
+    new_momentum = mine.astype(f32) - momentum_keep * feedback
     new_weights = (weights.astype(f32) - learn_rate * jnp.sqrt(M / N) * update).astype(bf16)
     return (new_weights, new_momentum[None], new_right)
 

time: 212 us -> 203 us (0.958)
  blocking collectives: 85.8 us -> 64.1 us
  waiting for transfers between devices: 24.9 us -> 38.5 us
  starting transfers between devices: 36.9 us -> 43.5 us
  Pallas kernels: 26.2 us -> 21.9 us
  matrix products: 17.6 us -> 14.6 us
    all_to_all x5 -> x4, blocking collectives: 85.8 us -> 64.1 us  [exchange(): return lax.all_to_all(value, axes, 0, 0, tiled=True)]
    all_to_all x3 -> x4, waiting for transfers between devices: 9.52 us -> 23.2 us  [exchange(): return lax.all_to_all(value, axes, 0, 0, tiled=True)]
    all_to_all x3 -> x4, starting transfers between devices: 13.2 us -> 19.5 us  [exchange(): return lax.all_to_all(value, axes, 0, 0, tiled=True)]
    pallas_call x2, Pallas kernels: 26.2 us -> 21.9 us  [half_factor(): pl.pallas_call(kernel, out_shape=jax.ShapeDtypeStruct((size, size), f32),...]
    dot_general x2 -> x1, matrix products: 4.87 us -> 2.14 us  [per_device(): left = jnp.dot(pair, right_half, preferred_element_type=f32)]
  transfers between devices with their start and end apart: 14 -> 15, of which waited for: 6 -> 7; matrix products, arithmetic and copies ran while one was open for 7% -> 7% of each run, Pallas kernels for 12% -> 11%
where the time goes in v2:
time: 203 us; the launch traced here: 202 us
  blocking collectives  64.1 us (32%)
  starting transfers between devices  43.5 us (21%)
  waiting for transfers between devices  38.5 us (19%)
  Pallas kernels  21.9 us (11%)
  matrix products  14.6 us (7%)
  other arithmetic  12.2 us (6%)
  local copies, waits for them, and re-layouts  5.94 us (3%)
    all_to_all x4, blocking collectives, exchange(): return lax.all_to_all(value, axes, 0, 0, tiled=True)  64.1 us
    all_to_all x4, waiting for transfers between devices, exchange(): return lax.all_to_all(value, axes, 0, 0, tiled=True)  23.2 us
    pallas_call x2, Pallas kernels, half_factor(): pl.pallas_call(kernel, out_shape=jax.ShapeDtypeStruct((size, size), f32),...  21.9 us
    all_to_all x4, starting transfers between devices, exchange(): return lax.all_to_all(value, axes, 0, 0, tiled=True)  19.5 us
    ppermute x7, waiting for transfers between devices, per_device(): lax.ppermute(term, 'z', [(n, (n + shift) % depth) for n in range(depth)])  14.2 us
    ppermute x4, starting transfers between devices, partner(): return lax.ppermute(value, 'c', SWAP)  12.8 us
    ppermute x7, starting transfers between devices, per_device(): lax.ppermute(term, 'z', [(n, (n + shift) % depth) for n in range(depth)])  11.1 us
    dot_general x5, matrix products, exact_dot(): lax.dot_general(a, b, dims, precision=precision, preferred_element_type=f32)  7 us
  transfers between devices with their start and end apart: 15, of which 7 were waited for; matrix products, arithmetic and copies ran while one was open for 7% of the time, Pallas kernels for 11%

profile of v2, /device:TPU:1, one launch (start us, length us, event | category | flops | bytes accessed | tf_op | source)
XLA Modules:
  0.0 201.7 jit_solution(6263602126659900791)
XLA Ops:
  0.6 0.0 copy-start
  0.6 3.3 %fusion.2 = bf16[448,2048]{1,0:T(8,128)(2,1)S(1)} fusion(f32[1,448,2048]{2,1,0:T(8,128)} %param.5, bf16[1,448,2048]{2,1,0:T(8,128)(2,1)} %param.6), kind=kLoop, calls=%fused_computation.9 | loop fusion | flops 2752512 | bytes 7340032 | tf_op jit(solution)/shard_map/convert_element_type | solution.py:158
  3.9 3.3 %collective-permute-start = (bf16[448,2048]{1,0:T(8,128)(2,1)S(1)}, bf16[448,2048]{1,0:T(8,128)(2,1)}, u32[]{:S(2)}, u32[]{:S(2)}) collective-permute-start(bf16[448,2048]{1,0:T(8,128)(2,1)S(1)} %fusion.2), channel_id=1, source_target_pairs={{0,16},{16,0},{1,17},{17,1},{2,18},{18,2},{3,19},{19,3},{4,20},{20... | collective-permute-start | bytes 5505032 | tf_op jit(solution)/shard_map/ppermute | solution.py:135
  7.2 0.0 copy-done
  7.2 1.1 broadcast_in_dim.12
  8.3 5.0 %all-to-all-start = ((bf16[16,128,256]{2,1,0:T(8,128)(2,1)}), bf16[16,128,256]{2,1,0:T(8,128)(2,1)S(1)}, u32[]{:S(2)}, u32[]{:S(2)}) async-start(bf16[16,128,256]{2,1,0:T(8,128)(2,1)} %broadcast_in_dim.12), calls=%async_computation | async-start | bytes 2097152 | tf_op jit(solution)/shard_map/all_to_all | solution.py:126
  13.3 0.0 collective-permute-done
  13.4 3.5 %fusion = bf16[448,2048]{1,0:T(8,128)(2,1)} fusion(bf16[448,2048]{1,0:T(8,128)(2,1)S(1)} %fusion.2, bf16[448,2048]{1,0:T(8,128)(2,1)} %collective-permute-done), kind=kLoop, calls=%fused_computation.4 | loop fusion | flops 3670016 | bytes 5505024 | tf_op jit(solution)/shard_map/convert_element_type | solution.py:161
  16.9 13.7 %all-to-all-done = bf16[16,128,256]{2,1,0:T(8,128)(2,1)S(1)} async-done(((bf16[16,128,256]{2,1,0:T(8,128)(2,1)}), bf16[16,128,256]{2,1,0:T(8,128)(2,1)S(1)}, u32[]{:S(2)}, u32[]{:S(2)}) %all-to-all-start) | async-done | bytes 1048608 | tf_op jit(solution)/shard_map/all_to_all | solution.py:126
  30.5 2.1 %convolution_convert_fusion.1 = bf16[448,256]{1,0:T(8,128)(2,1)S(1)} fusion(bf16[448,2048]{1,0:T(8,128)(2,1)} %fusion, bf16[2048,256]{1,0:T(8,128)(2,1)S(1)} %bitcast.45), kind=kOutput, calls=%fused_computation.11 | convolution fusion | flops 469876736 | bytes 3112960 | tf_op jit(solution)/shard_map/dot_general | solution.py:162
  32.7 16.9 %all_to_all.40 = bf16[8,56,256]{2,1,0:T(8,128)(2,1)S(1)} all-to-all(bf16[8,56,256]{2,1,0:T(8,128)(2,1)S(1)} %bitcast.46), channel_id=1, replica_groups=mesh['z'=8,'c'=2,'y'=4,'x'=4] {'z'}, dimensions={0} | all-to-all | bytes 458752 | tf_op jit(solution)/shard_map/all_to_all | solution.py:126
  49.6 14.7 %all_to_all.41 = f32[8,56,256]{2,1,0:T(8,128)S(1)} all-to-all(f32[8,56,256]{2,1,0:T(8,128)S(1)} %broadcast_in_dim.13), channel_id=1, replica_groups=mesh['z'=8,'c'=2,'y'=4,'x'=4] {'z'}, dimensions={0} | all-to-all | bytes 917504 | tf_op jit(solution)/shard_map/all_to_all | solution.py:126
  64.3 4.8 %collective-permute-start.1 = (f32[448,256]{1,0:T(8,128)S(1)}, f32[448,256]{1,0:T(8,128)}, u32[]{:S(2)}, u32[]{:S(2)}) collective-permute-start(f32[448,256]{1,0:T(8,128)S(1)} %bitcast.39), channel_id=1, source_target_pairs={{0,16},{16,0},{1,17},{17,1},{2,18},{18,2},{3,19},{19,3},{4,20},{20... | collective-permute-start | bytes 1376264 | tf_op jit(solution)/shard_map/ppermute | solution.py:135
  69.1 1.0 convolution_bitcast_fusion
  70.1 0.6 collective-permute-done.1
  70.7 1.1 broadcast_select_fusion
  71.8 0.0 copy-start.2
  71.8 0.6 fusion.19
  72.5 0.9 copy.8
  73.4 5.1 %all-to-all-start.3 = ((f32[16,16,384]{2,1,0:T(8,128)}), f32[16,16,384]{2,1,0:T(8,128)S(1)}, u32[]{:S(2)}, u32[]{:S(2)}) async-start(f32[16,16,384]{2,1,0:T(8,128)} %bitcast.43), calls=%async_computation.3 | async-start | bytes 786432 | tf_op jit(solution)/shard_map/all_to_all | solution.py:126
  78.5 9.5 %all-to-all-done.3 = f32[16,16,384]{2,1,0:T(8,128)S(1)} async-done(((f32[16,16,384]{2,1,0:T(8,128)}), f32[16,16,384]{2,1,0:T(8,128)S(1)}, u32[]{:S(2)}, u32[]{:S(2)}) %all-to-all-start.3) | async-done | bytes 393248 | tf_op jit(solution)/shard_map/all_to_all | solution.py:126
  88.1 0.8 broadcast_in_dim.14
  88.9 3.6 %all-to-all-start.4 = ((f32[16,16,384]{2,1,0:T(8,128)}), f32[16,16,384]{2,1,0:T(8,128)S(1)}, u32[]{:S(2)}, u32[]{:S(2)}) async-start(f32[16,16,384]{2,1,0:T(8,128)} %broadcast_in_dim.14), calls=%async_computation.4 | async-start | bytes 786432 | tf_op jit(solution)/shard_map/all_to_all | solution.py:126
  92.5 2.1 %constant_dynamic-slice_fusion = (bf16[448,128]{1,0:T(8,128)(2,1)}, bf16[448,128]{1,0:T(8,128)(2,1)}, bf16[448,128]{1,0:T(8,128)(2,1)}, bf16[448,128]{1,0:T(8,12...) fusion(bf16[448,2048]{1,0:T(8,128)(2,1)} %fusion, ...), kind=kLoop, calls=%fused_computation.47 | loop fusion | bytes 1835040 | tf_op jit(solution)/shard_map/dynamic_slice | solution.py:186
  94.6 0.3 collective-permute-start.3
  94.9 0.1 collective-permute-start.4
  95.0 2.0 collective-permute-start.5
  97.0 3.3 %collective-permute-start.6 = (bf16[448,128]{1,0:T(8,128)(2,1)}, bf16[448,128]{1,0:T(8,128)(2,1)}, u32[]{:S(2)}, u32[]{:S(2)}) collective-permute-start(bf16[448,128]{1,0:T(8,128)(2,1)} %get-tuple-element.21), channel_id=1, source_target_pairs={{0,128},{32,160},{64,192},{96,224},{128,0},{160,32},{192,64},{224,... | collective-permute-start | bytes 344072 | tf_op jit(solution)/shard_map/ppermute | solution.py:189
  100.3 0.9 collective-permute-start.7
  101.2 0.0 collective-permute-done.3
  101.3 2.9 %collective-permute-start.8 = (bf16[448,128]{1,0:T(8,128)(2,1)}, bf16[448,128]{1,0:T(8,128)(2,1)}, u32[]{:S(2)}, u32[]{:S(2)}) collective-permute-start(bf16[448,128]{1,0:T(8,128)(2,1)} %get-tuple-element.23), channel_id=1, source_target_pairs={{0,192},{32,224},{64,0},{96,32},{128,64},{160,96},{192,128},{224,1... | collective-permute-start | bytes 344072 | tf_op jit(solution)/shard_map/ppermute | solution.py:189
  104.1 0.0 collective-permute-done.4
  104.1 1.6 collective-permute-start.9
  105.7 0.0 copy-done.4
  105.7 7.7 %collective-permute-done.5 = bf16[448,128]{1,0:T(8,128)(2,1)} collective-permute-done((bf16[448,128]{1,0:T(8,128)(2,1)S(1)}, bf16[448,128]{1,0:T(8,128)(2,1)}, u32[]{:S(2)}, u32[]{:S(2)}) %collective-permute-start.5) | collective-permute-done | bytes 114720 | tf_op jit(solution)/shard_map/ppermute | solution.py:189
  113.4 0.0 all-to-all-done.4
  113.4 2.0 collective-permute-start.2
  115.4 0.0 collective-permute-done.6
  115.4 0.0 collective-permute-done.7
  115.4 3.5 %collective-permute-done.8 = bf16[448,128]{1,0:T(8,128)(2,1)} collective-permute-done((bf16[448,128]{1,0:T(8,128)(2,1)}, bf16[448,128]{1,0:T(8,128)(2,1)}, u32[]{:S(2)}, u32[]{:S(2)}) %collective-permute-start.8) | collective-permute-done | bytes 114720 | tf_op jit(solution)/shard_map/ppermute | solution.py:189
  118.9 3.0 %collective-permute-done.9 = bf16[448,128]{1,0:T(8,128)(2,1)} collective-permute-done((bf16[448,128]{1,0:T(8,128)(2,1)}, bf16[448,128]{1,0:T(8,128)(2,1)}, u32[]{:S(2)}, u32[]{:S(2)}) %collective-permute-start.9) | collective-permute-done | bytes 114720 | tf_op jit(solution)/shard_map/ppermute | solution.py:189
  121.9 1.8 convolution_bitcast_fusion.1
  123.7 13.8 %all_to_all.42 = f32[16,8,512]{2,1,0:T(8,128)S(1)} all-to-all(f32[16,8,512]{2,1,0:T(8,128)S(1)} %convolution_bitcast_fusion.1), channel_id=1, replica_groups=mesh['z'=8,'c'=2,'y'=4,'x'=4] {'y','x'}, dimensions={0} | all-to-all | bytes 524288 | tf_op jit(solution)/shard_map/all_to_all | solution.py:126
  137.6 0.7 broadcast_in_dim.15
  138.2 5.8 %all-to-all-start.6 = ((f32[8,8,512]{2,1,0:T(8,128)}), f32[8,8,512]{2,1,0:T(8,128)}, u32[]{:S(2)}, u32[]{:S(2)}) async-start(f32[8,8,512]{2,1,0:T(8,128)} %broadcast_in_dim.15), calls=%async_computation.6 | async-start | bytes 262144 | tf_op jit(solution)/shard_map/all_to_all | solution.py:126
  144.0 0.0 collective-permute-done.2
  144.0 1.1 broadcast_select_fusion.2
  145.1 11.4 %shard_map.67.in_ref = f32[512,512]{1,0:T(8,128)S(1)} custom-call(f32[256,384]{1,0:T(8,128)S(1)} %get-tuple-element.46.first_ref, f32[256,384]{1,0:T(8,128)S(1)} %get-tuple-element.45.second_ref), custom_call_target="tpu_custom_call" | custom-call | flops 6000000000 | bytes 2000000 | tf_op jit(solution)/shard_map/pallas_call | solution.py:113
  156.5 10.6 %shard_map.68 = f32[512,512]{1,0:T(8,128)S(1)} custom-call(f32[512,512]{1,0:T(8,128)S(1)} %shard_map.67.in_ref), custom_call_target="tpu_custom_call" | custom-call | flops 6000000000 | bytes 2000000 | tf_op jit(solution)/shard_map/pallas_call | solution.py:113
  167.0 0.0 all-to-all-done.6
  167.0 1.5 convolution_convert_fusion.2
  168.6 0.1 broadcast_in_dim.16
  168.7 18.7 %all_to_all.43 = bf16[16,64,512]{2,1,0:T(8,128)(2,1)} all-to-all(bf16[16,64,512]{2,1,0:T(8,128)(2,1)S(1)} %broadcast_in_dim.16), channel_id=1, replica_groups=mesh['z'=8,'c'=2,'y'=4,'x'=4] {'y','x'}, dimensions={0} | all-to-all | bytes 2097152 | tf_op jit(solution)/shard_map/all_to_all | solution.py:126
  187.4 2.8 %collective-permute-start.10 = (bf16[16,64,512]{2,1,0:T(8,128)(2,1)}, bf16[16,64,512]{2,1,0:T(8,128)(2,1)}, u32[]{:S(2)}, u32[]{:S(2)}) collective-permute-start(bf16[16,64,512]{2,1,0:T(8,128)(2,1)} %all_to_all.43), channel_id=1, source_target_pairs={{0,16},{16,0},{1,17},{17,1},{2,18},{18,2},{3,19},{19,3},{4,20},{20... | collective-permute-start | bytes 3145736 | tf_op jit(solution)/shard_map/ppermute | solution.py:135
  190.2 2.1 %convolution_convert_fusion = bf16[448,512]{1,0:T(8,128)(2,1)S(1)} fusion(f32[512,512]{1,0:T(8,128)S(1)} %shard_map.68, f32[448,256]{1,0:T(8,128)} %copy-done.2, f32[448,256]{1,0:T(8,128)} %copy-done.1), kind=kOutput, calls=%fused_computation.10 | convolution fusion | flops 705101824 | bytes 2424832 | tf_op jit(solution)/shard_map/dot_general | solution.py:69
  192.3 0.5 collective-permute-done.10
  192.8 1.7 select_bitcast_fusion.1
  194.5 0.6 multiply_reduce_fusion
  195.0 0.2 maximum_bitcast_fusion
  195.2 0.2 copy.9
  195.5 0.0 copy-start.5
  195.5 3.0 %fusion.1 = f32[1,448,2048]{2,1,0:T(8,128)} fusion(bf16[448,2048]{1,0:T(8,128)(2,1)S(1)} %fusion.2, bf16[448,512]{1,0:T(8,128)(2,1)S(1)} %convolution_convert_fusion, bf16[2048,512]{1,0:T(8,128)(2,1)S(1)} %bitcast.40), kind=kOutput, calls=%fused_computation.5 | convolution fusion | flops 942276608 | bytes 8060928 | tf_op jit(solution)/shard_map/dot_general | solution.py:213
  198.5 0.7 convert_divide_fusion
  199.2 2.5 %subtract_convert_fusion = bf16[448,2048]{1,0:T(8,128)(2,1)} fusion(bf16[448,2048]{1,0:T(8,128)(2,1)S(1)} %copy-done.5, bf16[448,512]{1,0:T(8,128)(2,1)S(1)} %convolution_convert_fusion, bf16[2048,512]{1,0:T(8,128)(2,1)S(1)} %bitcast.42, f32[512]{0:T(512)S(1)} %add_sqrt_fusion), kind=kOutput, calls=%fused_computation.6 | convolution fusion | flops 946339840 | bytes 6227968 | tf_op jit(solution)/shard_map/dot_general | solution.py:214
  (15 shorter events, 0.2 us)
Async XLA Ops:
  0.6 6.6 %copy-start = (f32[128,512]{1,0:T(8,128)S(1)}, f32[128,512]{1,0:T(8,128)}, u32[]{:S(2)}) copy-start(f32[128,512]{1,0:T(8,128)} %param.7) | copy-start | bytes 786436
  3.9 9.4 %collective-permute-start = (bf16[448,2048]{1,0:T(8,128)(2,1)S(1)}, bf16[448,2048]{1,0:T(8,128)(2,1)}, u32[]{:S(2)}, u32[]{:S(2)}) collective-permute-start(bf16[448,2048]{1,0:T(8,128)(2,1)S(1)} %fusion.2), channel_id=1, source_target_pairs={{0,16},{16,0},{1,17},{17,1},{2,18},{18,2},{3,19},{19,3},{4,20},{20... | collective-permute-start | bytes 5505032 | tf_op jit(solution)/shard_map/ppermute | solution.py:135
  8.3 22.3 %all-to-all-start = ((bf16[16,128,256]{2,1,0:T(8,128)(2,1)}), bf16[16,128,256]{2,1,0:T(8,128)(2,1)S(1)}, u32[]{:S(2)}, u32[]{:S(2)}) async-start(bf16[16,128,256]{2,1,0:T(8,128)(2,1)} %broadcast_in_dim.12), calls=%async_computation | async-start | bytes 2097152 | tf_op jit(solution)/shard_map/all_to_all | solution.py:126
  64.3 6.3 %collective-permute-start.1 = (f32[448,256]{1,0:T(8,128)S(1)}, f32[448,256]{1,0:T(8,128)}, u32[]{:S(2)}, u32[]{:S(2)}) collective-permute-start(f32[448,256]{1,0:T(8,128)S(1)} %bitcast.39), channel_id=1, source_target_pairs={{0,16},{16,0},{1,17},{17,1},{2,18},{18,2},{3,19},{19,3},{4,20},{20... | collective-permute-start | bytes 1376264 | tf_op jit(solution)/shard_map/ppermute | solution.py:135
  71.8 50.2 %copy-start.1 = (f32[448,256]{1,0:T(8,128)}, f32[448,256]{1,0:T(8,128)S(1)}, u32[]{:S(2)}) copy-start(f32[448,256]{1,0:T(8,128)S(1)} %get-tuple-element.44) | copy-start | bytes 1376260
  71.8 73.3 %copy-start.2 = (f32[448,256]{1,0:T(8,128)}, f32[448,256]{1,0:T(8,128)S(1)}, u32[]{:S(2)}) copy-start(f32[448,256]{1,0:T(8,128)S(1)} %get-tuple-element.43) | copy-start | bytes 1376260
  73.4 14.7 %all-to-all-start.3 = ((f32[16,16,384]{2,1,0:T(8,128)}), f32[16,16,384]{2,1,0:T(8,128)S(1)}, u32[]{:S(2)}, u32[]{:S(2)}) async-start(f32[16,16,384]{2,1,0:T(8,128)} %bitcast.43), calls=%async_computation.3 | async-start | bytes 786432 | tf_op jit(solution)/shard_map/all_to_all | solution.py:126
  88.9 24.6 %all-to-all-start.4 = ((f32[16,16,384]{2,1,0:T(8,128)}), f32[16,16,384]{2,1,0:T(8,128)S(1)}, u32[]{:S(2)}, u32[]{:S(2)}) async-start(f32[16,16,384]{2,1,0:T(8,128)} %broadcast_in_dim.14), calls=%async_computation.4 | async-start | bytes 786432 | tf_op jit(solution)/shard_map/all_to_all | solution.py:126
  94.6 6.7 %collective-permute-start.3 = (bf16[448,128]{1,0:T(8,128)(2,1)S(1)}, bf16[448,128]{1,0:T(8,128)(2,1)S(1)}, u32[]{:S(2)}, u32[]{:S(2)}) collective-permute-start(bf16[448,128]{1,0:T(8,128)(2,1)S(1)} %get-tuple-element.18), channel_id=1, source_target_pairs={{0,32},{32,64},{64,96},{96,128},{128,160},{160,192},{192,224},{224... | collective-permute-start | bytes 344072 | tf_op jit(solution)/shard_map/ppermute | solution.py:189
  94.9 9.2 %collective-permute-start.4 = (bf16[448,128]{1,0:T(8,128)(2,1)S(1)}, bf16[448,128]{1,0:T(8,128)(2,1)S(1)}, u32[]{:S(2)}, u32[]{:S(2)}) collective-permute-start(bf16[448,128]{1,0:T(8,128)(2,1)S(1)} %get-tuple-element.19), channel_id=1, source_target_pairs={{0,64},{32,96},{64,128},{96,160},{128,192},{160,224},{192,0},{224,... | collective-permute-start | bytes 344072 | tf_op jit(solution)/shard_map/ppermute | solution.py:189
  95.0 18.4 %collective-permute-start.5 = (bf16[448,128]{1,0:T(8,128)(2,1)S(1)}, bf16[448,128]{1,0:T(8,128)(2,1)}, u32[]{:S(2)}, u32[]{:S(2)}) collective-permute-start(bf16[448,128]{1,0:T(8,128)(2,1)S(1)} %get-tuple-element.20), channel_id=1, source_target_pairs={{0,96},{32,128},{64,160},{96,192},{128,224},{160,0},{192,32},{224,... | collective-permute-start | bytes 344072 | tf_op jit(solution)/shard_map/ppermute | solution.py:189
  97.0 18.4 %collective-permute-start.6 = (bf16[448,128]{1,0:T(8,128)(2,1)}, bf16[448,128]{1,0:T(8,128)(2,1)}, u32[]{:S(2)}, u32[]{:S(2)}) collective-permute-start(bf16[448,128]{1,0:T(8,128)(2,1)} %get-tuple-element.21), channel_id=1, source_target_pairs={{0,128},{32,160},{64,192},{96,224},{128,0},{160,32},{192,64},{224,... | collective-permute-start | bytes 344072 | tf_op jit(solution)/shard_map/ppermute | solution.py:189
  100.3 15.1 %collective-permute-start.7 = (bf16[448,128]{1,0:T(8,128)(2,1)}, bf16[448,128]{1,0:T(8,128)(2,1)}, u32[]{:S(2)}, u32[]{:S(2)}) collective-permute-start(bf16[448,128]{1,0:T(8,128)(2,1)} %get-tuple-element.22), channel_id=1, source_target_pairs={{0,160},{32,192},{64,224},{96,0},{128,32},{160,64},{192,96},{224,1... | collective-permute-start | bytes 344072 | tf_op jit(solution)/shard_map/ppermute | solution.py:189
  101.2 4.5 %copy-start.3 = (bf16[448,128]{1,0:T(8,128)(2,1)}, bf16[448,128]{1,0:T(8,128)(2,1)S(1)}, u32[]{:S(2)}) copy-start(bf16[448,128]{1,0:T(8,128)(2,1)S(1)} %collective-permute-done.3) | copy-start | bytes 344068
  101.3 17.7 %collective-permute-start.8 = (bf16[448,128]{1,0:T(8,128)(2,1)}, bf16[448,128]{1,0:T(8,128)(2,1)}, u32[]{:S(2)}, u32[]{:S(2)}) collective-permute-start(bf16[448,128]{1,0:T(8,128)(2,1)} %get-tuple-element.23), channel_id=1, source_target_pairs={{0,192},{32,224},{64,0},{96,32},{128,64},{160,96},{192,128},{224,1... | collective-permute-start | bytes 344072 | tf_op jit(solution)/shard_map/ppermute | solution.py:189
  104.1 1.6 copy-start.4
  104.1 17.8 %collective-permute-start.9 = (bf16[448,128]{1,0:T(8,128)(2,1)}, bf16[448,128]{1,0:T(8,128)(2,1)}, u32[]{:S(2)}, u32[]{:S(2)}) collective-permute-start(bf16[448,128]{1,0:T(8,128)(2,1)} %get-tuple-element.24), channel_id=1, source_target_pairs={{0,224},{32,0},{64,32},{96,64},{128,96},{160,128},{192,160},{224,1... | collective-permute-start | bytes 344072 | tf_op jit(solution)/shard_map/ppermute | solution.py:189
  113.4 30.6 %collective-permute-start.2 = (f32[256,384]{1,0:T(8,128)S(1)}, f32[256,384]{1,0:T(8,128)}, u32[]{:S(2)}, u32[]{:S(2)}) collective-permute-start(f32[256,384]{1,0:T(8,128)S(1)} %bitcast.44), channel_id=1, source_target_pairs={{0,16},{16,0},{1,17},{17,1},{2,18},{18,2},{3,19},{19,3},{4,20},{20... | collective-permute-start | bytes 1179656 | tf_op jit(solution)/shard_map/ppermute | solution.py:135
  138.2 28.8 %all-to-all-start.6 = ((f32[8,8,512]{2,1,0:T(8,128)}), f32[8,8,512]{2,1,0:T(8,128)}, u32[]{:S(2)}, u32[]{:S(2)}) async-start(f32[8,8,512]{2,1,0:T(8,128)} %broadcast_in_dim.15), calls=%async_computation.6 | async-start | bytes 262144 | tf_op jit(solution)/shard_map/all_to_all | solution.py:126
  187.4 5.4 %collective-permute-start.10 = (bf16[16,64,512]{2,1,0:T(8,128)(2,1)}, bf16[16,64,512]{2,1,0:T(8,128)(2,1)}, u32[]{:S(2)}, u32[]{:S(2)}) collective-permute-start(bf16[16,64,512]{2,1,0:T(8,128)(2,1)} %all_to_all.43), channel_id=1, source_target_pairs={{0,16},{16,0},{1,17},{17,1},{2,18},{18,2},{3,19},{19,3},{4,20},{20... | collective-permute-start | bytes 3145736 | tf_op jit(solution)/shard_map/ppermute | solution.py:135
  195.5 3.7 %copy-start.5 = (bf16[448,2048]{1,0:T(8,128)(2,1)S(1)}, bf16[448,2048]{1,0:T(8,128)(2,1)}, u32[]{:S(2)}) copy-start(bf16[448,2048]{1,0:T(8,128)(2,1)} %param.4) | copy-start | bytes 5505028
